TPU v7x, 512 devices: a whole 4x8x8 slice. The times are simulated.
512 devices in a mesh: dp: 32 (over x, y), seq: 16 (over z, core).
Axes of the slice: x: 4, y: 8, z: 8, core: 2. Of those that a mesh axis runs over, the one named last changes fastest.
Arguments:
- features: bfloat16 [32, 2048, 2560], P('dp', 'seq'), may hold values from -6 to 6
- head_inputs: bfloat16 [32, 2048, 2560], P('dp', 'seq'), may hold values from -6 to 6
- out_grad: bfloat16 [32, 2048, 2560], P('dp', 'seq'), may hold values from -6 to 6
- bc_weight: bfloat16 [2560, 128], P('dp'), may hold values from -0.125 to 0.125
- dt_weight: bfloat16 [2560, 40], P('dp'), may hold values from -0.125 to 0.125
- dt_bias: float32 [40], replicated, may hold values from -7 to -5.5
- decay_rate: float32 [40], replicated, may hold values from 0.078125 to 16
- skip_gain: float32 [40], replicated, may hold values from 0.5 to 1.5
Outputs:
- input_grad: bfloat16 [32, 2048, 2560], P('dp', 'seq')
- head_grad: bfloat16 [32, 2048, 2560], P('dp', 'seq')
- bc_weight_grad: float32 [2560, 128], P('dp')
- dt_weight_grad: float32 [2560, 40], P('dp')
All inputs are finite; a program needn't handle non-finite values.
Results may differ from a plain program's by a relative error of at most 0.0049.
Values may be sent and summed in bfloat16 or wider, within the bound.
No kernel may reach another device: no remote copies, remote signals or barrier semaphores. Data moves between devices by JAX's collectives and lax.ppermute only.
A program may use at most 128 MiB of HBM per device.

v0:
```python
import math

import jax
import jax.numpy as jnp
from jax import lax
from jax.sharding import PartitionSpec as P

highest = lax.Precision.HIGHEST


def entering(value, axis, join, neutral, backward):
    count, mine = (lax.axis_size(axis), lax.axis_index(axis))
    pieces = jax.tree.map(lambda part: lax.all_gather(part, axis), value)
    if backward:
        pieces = jax.tree.map(lambda part: part[::-1], pieces)
        mine = count - 1 - mine
    total = jax.tree.map(
        lambda part, zero: jnp.full_like(part, 0) + jnp.asarray(zero, part.dtype), value, neutral
    )

    def hop(position, total):
        longer = join(total, jax.tree.map(lambda part: part[position], pieces))
        return jax.tree.map(lambda new, old: jnp.where(position < mine, new, old), longer, total)

    return lax.fori_loop(0, count - 1, hop, total)


def spread_heads(values, head_size):
    return jnp.repeat(values, head_size, axis=-1)


def chain_link(earlier, later):
    decay_one, state_one = earlier
    decay_two, state_two = later
    head_size = state_one.shape[1] // decay_one.shape[0]
    factor = spread_heads(jnp.exp(decay_two), head_size)
    return (decay_one + decay_two, state_one * factor[None, :] + state_two)


def body(features, head_inputs, out_grad, bc_weight, dt_weight, dt_bias, decay_rate, skip_gain):
    tokens = features[0]
    inputs_f = head_inputs[0].astype(jnp.float32)
    cotangent = out_grad[0].astype(jnp.float32)
    heads = dt_bias.shape[0]
    inner = inputs_f.shape[1]
    head_size = inner // heads
    state = bc_weight.shape[1] // 2
    length = tokens.shape[0]
    joined = jnp.concatenate([bc_weight, dt_weight], axis=1)
    columns = tokens
    projection = jnp.dot(
        columns,
        lax.all_gather(joined, "dp", axis=0, tiled=True),
        preferred_element_type=jnp.float32,
    )
    b_rows = projection[:, :state]
    c_rows = projection[:, state : 2 * state]
    pre_step = projection[:, 2 * state :] + dt_bias[None, :]
    step_size = jax.nn.softplus(pre_step)
    log_decay = -decay_rate[None, :] * step_size
    cumulative = jnp.cumsum(log_decay, axis=0)
    total_decay = cumulative[-1]
    scaled_in = inputs_f * spread_heads(step_size, head_size)
    to_end = jnp.exp(total_decay[None, :] - cumulative)
    end_weight = spread_heads(to_end, head_size)
    scaled_end = scaled_in * end_weight
    local_state = jnp.dot(b_rows.T, scaled_end, precision=highest)
    from_start = jnp.exp(cumulative)
    weighted_grad = cotangent * spread_heads(from_start, head_size)
    returned_part = jnp.dot(c_rows.T, weighted_grad, precision=highest)
    identity = (jnp.zeros_like(total_decay), jnp.zeros_like(local_state))
    carried = entering((total_decay, local_state), "seq", chain_link, identity, False)
    returned = entering((total_decay, returned_part), "seq", chain_link, identity, True)
    state_in = carried[1]
    state_grad = returned[1]
    positions = jnp.arange(length)
    causal = positions[:, None] >= positions[None, :]
    gap = cumulative.T[:, :, None] - cumulative.T[:, None, :]
    weights_mat = jnp.exp(jnp.where(causal[None], gap, -1e30))
    intersection = jnp.dot(c_rows, b_rows.T, precision=highest)
    mixing = intersection[None] * weights_mat
    grad_view = cotangent.reshape(length, heads, head_size)
    input_view = scaled_in.reshape(length, heads, head_size)
    mixing_grad = jnp.einsum("thp,uhp->htu", grad_view, input_view, precision=highest)
    intersection_grad = jnp.sum(mixing_grad * weights_mat, axis=0)
    product = mixing_grad * mixing
    cum_grad = (jnp.sum(product, axis=2) - jnp.sum(product, axis=1)).T
    c_grad = jnp.dot(intersection_grad, b_rows, precision=highest)
    b_grad = jnp.dot(intersection_grad.T, c_rows, precision=highest)
    scaled_grad = jnp.einsum("htu,thp->uhp", mixing, grad_view, precision=highest).reshape(
        length, inner
    )
    inter_out = jnp.dot(c_rows, state_in, precision=highest)
    c_grad = c_grad + jnp.dot(weighted_grad, state_in.T, precision=highest)
    cum_grad = cum_grad + from_start * jnp.sum(
        (cotangent * inter_out).reshape(length, heads, head_size), axis=2
    )
    reach = jnp.dot(b_rows, state_grad, precision=highest)
    scaled_grad = scaled_grad + end_weight * reach
    b_grad = b_grad + jnp.dot(scaled_end, state_grad.T, precision=highest)
    to_end_grad = jnp.sum((scaled_in * reach).reshape(length, heads, head_size), axis=2) * to_end
    cum_grad = cum_grad - to_end_grad
    end_grad = jnp.sum(to_end_grad, axis=0) + jnp.exp(total_decay) * jnp.sum(
        (state_grad * state_in).reshape(state, heads, head_size), axis=(0, 2)
    )
    cum_grad = cum_grad.at[length - 1].add(end_grad)
    decay_grad = jnp.cumsum(cum_grad[::-1], axis=0)[::-1]
    step_grad = -decay_rate[None, :] * decay_grad + jnp.sum(
        (inputs_f * scaled_grad).reshape(length, heads, head_size), axis=2
    )
    pre_grad = step_grad * jax.nn.sigmoid(pre_step)
    head_grad = (
        cotangent * spread_heads(skip_gain, head_size)[None, :]
        + spread_heads(step_size, head_size) * scaled_grad
    ).astype(jnp.bfloat16)
    proj_grad = jnp.concatenate([b_grad, c_grad, pre_grad], axis=1).astype(jnp.bfloat16)
    input_grad = lax.dot_general(
        proj_grad,
        lax.all_gather(joined, "dp", axis=0, tiled=True),
        (((1,), (1,)), ((), ())),
        preferred_element_type=jnp.float32,
    )
    input_grad = input_grad.astype(jnp.bfloat16)
    columns = tokens
    owned = lax.psum_scatter(
        lax.dot_general(
            columns, proj_grad, (((0,), (0,)), ((), ())), preferred_element_type=jnp.float32
        ),
        "dp",
        scatter_dimension=0,
        tiled=True,
    )
    summed = lax.psum(owned, "seq")
    summed = summed * (1.0 / math.sqrt(lax.axis_size("dp") * lax.axis_size("seq") * length))
    return (input_grad[None], head_grad[None], summed[:, : 2 * state], summed[:, 2 * state :])


def solution(mesh):
    in_specs = (
        P("dp", "seq", None),
        P("dp", "seq", None),
        P("dp", "seq", None),
        P("dp", None),
        P("dp", None),
        P(),
        P(),
        P(),
    )
    out_specs = (P("dp", "seq", None), P("dp", "seq", None), P("dp", None), P("dp", None))
    return jax.shard_map(body, mesh=mesh, in_specs=in_specs, out_specs=out_specs, check_vma=False)
```

profile of v0, /device:TPU:16, one launch (start us, length us, event | category | flops | bytes accessed | tf_op | source)
XLA Modules:
  0.0 582.4 jit_solution(10673328906108149819)
XLA Ops:
  8.8 50.7 %all_gather.20 = bf16[2560,168]{1,0:T(8,128)(2,1)S(1)} all-gather(bf16[80,168]{1,0:T(8,128)(2,1)S(1)} %pad_maximum_fusion.1), channel_id=1, replica_groups=mesh['dp'=32,'seq'=16] {'dp'}, dimensions={0}, use_global_device_ids=true | all-gather | bytes 887040 | tf_op jit(solution)/shard_map/all_gather | solution.py:53
  62.8 1.8 copy.132
  66.6 23.1 %all-gather.2 = f32[16,1,40]{2,1,0:T(1,128)S(1)} all-gather(f32[1,1,40]{2,1,0:T(1,128)S(1)} %bitcast.111), channel_id=1, replica_groups=mesh['dp'=32,'seq'=16] {'seq'}, dimensions={0}, use_global_device_ids=true | all-gather | bytes 2720 | tf_op jit(solution)/shard_map/all_gather | solution.py:13
  90.9 1.8 copy.127
  92.7 45.2 %all-gather.6.cloned.1.call-done = f32[1024,2560]{1,0:T(8,128)} async-done(((f32[64,2560]{1,0:T(8,128)}), f32[1024,2560]{1,0:T(8,128)}) %all-gather.6.cloned.1.call-update) | async-done | bytes 10485776 | tf_op jit(solution)/shard_map/all_gather | solution.py:13
  137.9 8.8 %rev.13 = f32[16,64,2560]{2,1,0:T(8,128)} reverse(f32[16,64,2560]{2,1,0:T(8,128)} %bitcast.96), dimensions={0} | reverse | bytes 20971520 | tf_op jit(solution)/shard_map/rev | solution.py:15
  146.7 27.3 %while.29 = (s32[]{:T(128)}, f32[64,2560]{1,0:T(8,128)S(1)}, s32[]{:T(128)}, f32[16,40]{1,0:T(8,128)S(1)}, f32[16,64,2560]{2,1,0:T(8,128)}, /*index=5*/s32[]{:T(128)}, s32[]{:T(128)}) while((s32[]{:T(128)}, f32[64,2560]{1,0:T(8,128)S(1)}, s32[]{:T(128)}, f32[16,40]{1,0:T(8,128)S(1)}, f32[16,64,2560]{2,1,0:T(8,128)}, ...), condition=%wide.region_3.4_spmd.clone, body=%wide.region_2.3_spmd.clone.sunk | while | flops 655364 | bytes 2007625 | solution.py:25
  174.1 3.9 fusion.26
  178.0 2.8 copy.135
  184.1 2.8 copy.130
  187.0 3.3 fusion.29
  191.6 2.4 copy.121
  194.4 5.2 fusion.5
  199.6 2.8 copy.142
  202.5 5.8 fusion.7
  209.5 4.4 fusion.21
  214.0 2.8 copy.143
  216.7 2.1 reduce_sum.94
  218.8 3.0 fusion.18
  221.8 35.8 %all-gather.8.cloned.1.call-done = f32[1024,2560]{1,0:T(8,128)} async-done(((f32[64,2560]{1,0:T(8,128)}), f32[1024,2560]{1,0:T(8,128)}) %all-gather.8.cloned.1.call-update) | async-done | bytes 10485776 | tf_op jit(solution)/shard_map/all_gather | solution.py:13
  257.6 37.5 %while.30 = (s32[]{:T(128)}, f32[64,2560]{1,0:T(8,128)S(1)}, s32[]{:T(128)}, f32[16,40]{1,0:T(8,128)}, f32[16,64,2560]{2,1,0:T(8,128)}, /*index=5*/s32[]{:T(128)}, s32[]{:T(128)}) while((s32[]{:T(128)}, f32[64,2560]{1,0:T(8,128)S(1)}, s32[]{:T(128)}, f32[16,40]{1,0:T(8,128)}, f32[16,64,2560]{2,1,0:T(8,128)}, /*index=5*/s32[]{:T(128)}, ...), condition=%wide.region_5.6_spmd.clone, body=%wide.region_4.5_spmd.clone.sunk | while | flops 655364 | bytes 2007625 | solution.py:25
  303.6 2.0 copy.148
  308.4 217.5 %reduce-scatter.4.cloned.1.call-done = f32[80,168]{1,0:T(8,128)} async-done(((f32[2560,168]{1,0:T(8,128)}), f32[80,168]{1,0:T(8,128)}) %reduce-scatter.4.cloned.1.call-update) | async-done | bytes 53776
  526.9 47.6 %psum.7 = f32[80,168]{0,1:T(8,128)S(1)} all-reduce(f32[80,168]{0,1:T(8,128)S(1)} %copy.149), channel_id=1, replica_groups=mesh['dp'=32,'seq'=16] {'seq'}, use_global_device_ids=true, to_apply=%region_16.17 | all-reduce | flops 13440 | bytes 107520 | tf_op jit(solution)/shard_map/psum | solution.py:133
  (216 shorter events, 92.0 us)
Async XLA Ops:
  7.2 53.5 %copy-start = (bf16[1,128,2560]{2,1,0:T(8,128)(2,1)S(1)}, bf16[1,128,2560]{2,1,0:T(8,128)(2,1)}, u32[]{:S(2)}) copy-start(bf16[1,128,2560]{2,1,0:T(8,128)(2,1)} %param.14) | copy-start | bytes 1966084
  7.2 52.4 %copy-start.18 = (f32[40]{0:T(128)S(1)}, f32[40]{0:T(128)}, u32[]{:S(2)}) copy-start(f32[40]{0:T(128)} %param.20) | copy-start | bytes 484
  7.2 130.7 %all-gather.6.cloned.1.call-start = ((), (), s32[]{:S(2)}) async-start(), calls=%async_computation.1 | async-start | bytes 11141120 | tf_op jit(solution)/shard_map/all_gather | solution.py:13
  59.6 1.1 copy-start.3
  59.6 1.6 copy-start.13
  60.6 0.6 copy-start.15
  62.8 1.8 copy-start.1
  64.6 1.8 copy-start.5
  66.4 191.2 %all-gather.8.cloned.1.call-start = ((), (), s32[]{:S(2)}) async-start(), calls=%async_computation.2 | async-start | bytes 11141120 | tf_op jit(solution)/shard_map/all_gather | solution.py:13
  89.7 3.0 copy-start.8
  190.3 335.7 %reduce-scatter.4.cloned.1.call-start = ((), (), s32[]{:S(2)}) async-start(), calls=%async_computation.3 | async-start | bytes 2703360
  194.0 5.5 copy-start.11
  194.1 5.5 copy-start.12
  199.6 2.8 copy-start.17
  295.1 1.1 copy-start.2
  296.2 1.3 copy-start.6
  300.8 1.5 copy-start.9
  300.8 1.5 copy-start.10
  300.8 2.3 copy-start.7
  300.8 2.3 copy-start.14
  300.8 2.3 copy-start.16
  305.7 1.3 copy-start.4
Sparse Core Ops, SparseCore 0:
  66.5 71.3 all-gather.5
  190.4 67.2 all-gather.7
  305.8 220.0 reduce-scatter.3
where the time goes:
time: 585 us; the launch traced here: 582 us
  waiting for transfers between devices  299 us (51%)
  blocking collectives  121 us (21%)
  other arithmetic  61.2 us (10%)
  local copies, waits for them, and re-layouts  57.5 us (10%)
  matrix products  28.7 us (5%)
  between operations  14.1 us (2%)
    unnamed x4, waiting for transfers between devices  218 us
    all_gather x2, waiting for transfers between devices, entering(): pieces = jax.tree.map(lambda part: lax.all_gather(part, axis), value)  81.1 us
    all_gather x1, blocking collectives, body(): lax.all_gather(joined, 'dp', axis=0, tiled=True)  50.7 us
    select_n x30, other arithmetic, hop(): jnp.where(position < mine, new, old)  49.4 us
    psum x1, blocking collectives, body(): summed = lax.psum(owned, 'seq')  47.6 us
    all_gather x1, blocking collectives, entering(): pieces = jax.tree.map(lambda part: lax.all_gather(part, axis), value)  23.1 us
  transfers between devices with their start and end apart: 3, of which 3 were waited for; matrix products, arithmetic and copies ran while one was open for 6% of the time, Pallas kernels for 0%

commit v1 on v0

v1 whole, which is shorter than its diff:
```python
import math

import jax
import jax.numpy as jnp
from jax import lax
from jax.experimental import pallas as pl
from jax.experimental.pallas import tpu as pltpu
from jax.sharding import PartitionSpec as P

bf16, f32 = jnp.bfloat16, jnp.float32
highest = lax.Precision.HIGHEST

HEADS = 40
PAIRS = 20
TOK = 128
WIDE = 2560
ROWS = 80
DP = 32
SEQ = 16
HALF = 64
LANES = 128

NN = (((1,), (0,)), ((), ()))
NT = (((1,), (1,)), ((), ()))
TN = (((0,), (0,)), ((), ()))


def iota(shape, axis):
    return lax.broadcasted_iota(jnp.int32, shape, axis)


def ones_where(mask, dtype=f32):
    return jnp.where(mask, 1.0, 0.0).astype(dtype)


def mm(a, b, dims=NN):
    return lax.dot_general(a.astype(bf16), b.astype(bf16), dims, preferred_element_type=f32)


def high_low(value):
    high = value.astype(bf16)
    return high, (value - high.astype(f32)).astype(bf16)


def mm_exact(a, b, dims=NN):
    return lax.dot_general(a, b, dims, precision=highest, preferred_element_type=f32)


def head_of_lane(lane):
    return lane - jnp.where(lane >= 40, 40, 0) - jnp.where(lane >= 80, 40, 0)


def interleave(shape, source_axis):
    source, target = iota(shape, source_axis), iota(shape, 1 - source_axis)
    low = target & 7
    wanted = 4 * (target >> 3) + low + jnp.where(low >= 4, 60, 0)
    return ones_where(source == wanted)


def triple(row):
    place = ones_where(iota((HEADS, LANES), 0) == head_of_lane(iota((HEADS, LANES), 1)))
    return mm_exact(jnp.broadcast_to(row, (8, HEADS)), place)[0:1]


def split(value):
    lane = iota(value.shape, 1)
    first = value.astype(bf16).astype(f32)
    rest = value - first
    second = rest.astype(bf16).astype(f32)
    third = rest - second
    return jnp.where(lane < 40, first, jnp.where(lane < 80, second, third)).astype(bf16)


def spread_matrix(pair):
    k, lane = iota((LANES, LANES), 0), iota((LANES, LANES), 1)
    return ones_where(head_of_lane(k) == 2 * pair + (lane >> 6), bf16)


def gather_matrix(pair):
    lane, k = iota((LANES, LANES), 0), iota((LANES, LANES), 1)
    return ones_where(head_of_lane(k) == 2 * pair + (lane >> 6), bf16)


def pack_kernel(core_ref, bc_ref, dt_ref, out_ref):
    bc = mm(bc_ref[...], interleave((LANES, LANES), 0))
    row, lane = iota((HEADS, LANES), 0), iota((HEADS, LANES), 1)
    dt = dt_ref[...]
    packed = mm(dt[0:32], ones_where(lane == row)) + mm(dt[32:64], ones_where(lane == row + 40))
    last = mm(dt[64:80], ones_where(lane == row + 80))
    zeros = jnp.zeros((16, LANES), f32)
    packed = packed + jnp.concatenate([last, zeros], axis=0)
    second = jnp.concatenate([bc[64:80], packed, zeros], axis=0)
    value = jnp.where(core_ref[0] == 0, bc[0:64], second).astype(bf16)
    for owner in range(DP):
        out_ref[owner] = value


def first_kernel(
    core_ref, mine_ref, other_ref, feat_ref, x_ref, g_ref, bias_ref, rate_ref,
    weight_ref, proj_ref, pre_ref, cum_ref, state_ref,
):
    lane16 = iota((16, LANES), 1)
    group = [
        ones_where((lane16 >= 40 * k) & (lane16 < 40 * k + 40), bf16) for k in range(3)
    ]

    def assemble(one_ref, two_ref):
        for owner in range(DP):
            base = ROWS * owner
            weight_ref[base : base + 64, 0:LANES] = one_ref[owner]
            weight_ref[base + 64 : base + 80, 0:LANES] = two_ref[owner, 0:16, :]
            low, high = two_ref[owner, 16:32, :], two_ref[owner, 32:48, :]
            weight_ref[base : base + 16, LANES:] = low * group[0]
            weight_ref[base + 16 : base + 32, LANES:] = high * group[0]
            weight_ref[base + 32 : base + 48, LANES:] = low * group[1]
            weight_ref[base + 48 : base + 64, LANES:] = high * group[1]
            weight_ref[base + 64 : base + 80, LANES:] = low * group[2]

    core = core_ref[0]

    @pl.when(core == 0)
    def _():
        assemble(mine_ref, other_ref)

    @pl.when(core != 0)
    def _():
        assemble(other_ref, mine_ref)

    both = lax.dot_general(feat_ref[...], weight_ref[...], NN, preferred_element_type=f32)
    proj = both[:, 0:LANES]
    row, lane = iota((LANES, LANES), 0), iota((LANES, LANES), 1)
    head_row, head_lane = head_of_lane(row), head_of_lane(lane)
    fold = ones_where((head_row == head_lane) & (head_lane < HEADS))
    pre = mm_exact(both[:, LANES:], fold) + triple(bias_ref[...])
    step = jnp.maximum(pre, 0.0) + jnp.log1p(jnp.exp(-jnp.abs(pre)))
    cum = mm_exact(ones_where(row >= lane), -triple(rate_ref[...]) * step)
    proj_ref[...] = proj
    pre_ref[...] = pre
    cum_ref[...] = cum
    total = cum[TOK - 1 : TOK]
    stacked = jnp.concatenate(
        [split(step * jnp.exp(total - cum)), split(jnp.exp(cum))], axis=0
    )
    turned_high, turned_low = high_low(proj.T)
    both_turned = jnp.concatenate([turned_high, turned_low], axis=0)
    forward = (row & 7) < 4

    def block(pair):
        cols = slice(LANES * pair, LANES * pair + LANES)
        wide = lax.dot_general(stacked, spread_matrix(pair), NN, preferred_element_type=f32)
        ending = x_ref[:, cols].astype(f32) * wide[0:TOK]
        weighted = g_ref[:, cols].astype(f32) * wide[TOK:]
        high, low = high_low(jnp.concatenate([ending, weighted], axis=1))
        joined = mm(both_turned, high)
        joined = joined[0:LANES] + (joined[LANES:] + mm(turned_high, low))
        return jnp.where(forward, joined[:, 0:LANES], joined[:, LANES:]).reshape(SEQ, 8, LANES)

    for two in range(PAIRS // 2):
        value = jnp.concatenate([block(2 * two), block(2 * two + 1)], axis=1)
        state_ref[:, 16 * two : 16 * two + 16, :] = value.astype(bf16)
    decay = split(jnp.broadcast_to(total, (16, LANES)))
    for owner in range(SEQ):
        state_ref[owner, 160:176, :] = decay


def chain_kernel(state_ref, out_ref):
    row16 = iota((16, LANES), 0)
    logs = jnp.zeros((16, LANES), f32)
    for place in range(SEQ):
        logs = logs + jnp.where(row16 == place, state_ref[place, 160:176, :].astype(f32), 0.0)
    logs = logs.astype(bf16)
    forward = (row16 & 7) < 4
    for two in range(PAIRS // 2):
        rows = slice(16 * two, 16 * two + 16)
        factor = [
            jnp.exp(
                lax.dot_general(
                    logs, spread_matrix(2 * two + k), NN, preferred_element_type=f32
                )
            )
            for k in range(2)
        ]

        def decay(place):
            return jnp.concatenate(
                [jnp.broadcast_to(factor[k][place : place + 1], (8, LANES)) for k in range(2)],
                axis=0,
            )

        values = [state_ref[place, rows, :].astype(f32) for place in range(SEQ)]
        decays = [decay(place) for place in range(SEQ)]
        ahead = [jnp.zeros((16, LANES), f32)]
        for place in range(SEQ - 1):
            ahead.append(ahead[-1] * decays[place] + values[place])
        back = jnp.zeros((16, LANES), f32)
        for place in range(SEQ - 1, -1, -1):
            out_ref[place, rows, :] = jnp.where(forward, ahead[place], back).astype(bf16)
            back = back * decays[place] + values[place]


def softplus(pre):
    return jnp.maximum(pre, 0.0) + jnp.log1p(jnp.exp(-jnp.abs(pre)))


def inside_kernel(
    proj_ref, pre_ref, cum_ref, x_ref, g_ref, scaled_ref, across_ref, later_ref, own_ref, rows_ref
):
    proj, cum = proj_ref[...], cum_ref[...]
    step = softplus(pre_ref[...])
    row, lane = iota((LANES, LANES), 0), iota((LANES, LANES), 1)
    low = (lane & 7) < 4
    b_low = jnp.where(low, proj, 0.0)
    c_low = jnp.where(low, pltpu.roll(proj, LANES - 4, 1), 0.0)
    meet = mm_exact(b_low, c_low, NT)
    causal = lane >= row
    cum_turned = cum.T
    lane_head = head_of_lane(lane)
    across = jnp.zeros((TOK, TOK), f32)
    own = jnp.zeros((TOK, LANES), f32)
    first_half = ones_where(lane < 64, bf16)
    second_half = ones_where(lane >= 64, bf16)
    rows_ref[...] = jnp.zeros_like(rows_ref)
    for pair in range(PAIRS):
        cols = slice(LANES * pair, LANES * pair + LANES)
        x, g = x_ref[:, cols], g_ref[:, cols]
        mixed, parts = [], []
        for which, half in enumerate((first_half, second_half)):
            head = 2 * pair + which
            g_half = g * half
            outer = lax.dot_general(x, g_half, NT, preferred_element_type=f32)
            gap = cum_turned[head : head + 1, :] - cum[:, head : head + 1]
            weight = jnp.exp(jnp.where(causal, gap, -1e30))
            step_col = step[:, head : head + 1]
            spot = outer * weight
            across = across + spot * step_col
            product = spot * meet
            own = jnp.where(lane_head == head, jnp.sum(product, axis=1, keepdims=True), own)
            rows_ref[head : head + 1, :] = jnp.sum(product * step_col, axis=0, keepdims=True)
            mixed.append((meet * weight).astype(bf16))
            parts.append(g_half)
        scaled_ref[:, cols] = lax.dot_general(
            jnp.concatenate(mixed, axis=1), jnp.concatenate(parts, axis=0), NN,
            preferred_element_type=f32,
        )
    across_ref[...] = across
    own_ref[...] = own
    place = ones_where((row == lane_head) & (row < HEADS))
    later_ref[...] = mm_exact(rows_ref[...].T, place)


def last_kernel(
    core_ref, carried_ref, weight_ref, proj_ref, pre_ref, cum_ref, scaled_ref, across_ref,
    later_ref, own_ref, feat_ref, x_ref, g_ref, rate_ref, skip_ref,
    input_grad_ref, head_grad_ref, keep_ref, send_ref,
):
    proj, pre, cum = proj_ref[...], pre_ref[...], cum_ref[...]
    step = softplus(pre)
    total = cum[TOK - 1 : TOK]
    row, lane = iota((LANES, LANES), 0), iota((LANES, LANES), 1)
    low = (lane & 7) < 4
    c_low = jnp.where(low, pltpu.roll(proj, LANES - 4, 1), 0.0)
    b_high = jnp.where(low, 0.0, pltpu.roll(proj, 4, 1))
    left = jnp.concatenate([c_low, b_high], axis=0)
    left = jnp.concatenate(high_low(left), axis=0)
    stacked = jnp.concatenate(
        [
            split(step),
            split(jnp.exp(total - cum)),
            split(jnp.exp(cum)),
            split(jnp.broadcast_to(triple(skip_ref[...]), (16, LANES))),
        ],
        axis=0,
    )
    crossed = jnp.zeros((4 * TOK, LANES), f32)
    sums = jnp.zeros((4 * TOK + 32, LANES), f32)
    low_rows = (row & 7) < 4
    for two in range(PAIRS // 2):
        chunk = carried_ref[:, 16 * two : 16 * two + 16, :].astype(f32)
        for which in range(2):
            pair = 2 * two + which
            cols = slice(LANES * pair, LANES * pair + LANES)
            state = chunk[:, 8 * which : 8 * which + 8, :].reshape(LANES, LANES)
            state_b = state.astype(bf16)
            wide = lax.dot_general(stacked, spread_matrix(pair), NN, preferred_element_type=f32)
            step_w, end_w, start_w = wide[0:TOK], wide[TOK : 2 * TOK], wide[2 * TOK : 3 * TOK]
            skip_w = wide[3 * TOK : 3 * TOK + 1]
            x, g = x_ref[:, cols].astype(f32), g_ref[:, cols].astype(f32)
            weighted = g * start_w
            ending = x * end_w
            pushed = lax.dot_general(left, state_b, NN, preferred_element_type=f32)
            pushed = pushed[0 : 2 * TOK] + pushed[2 * TOK :]
            out, reach = pushed[0:TOK], pushed[TOK:]
            lines = jnp.concatenate([weighted, ending * step_w], axis=0)
            crossed = crossed + mm(jnp.concatenate(high_low(lines), axis=0), state_b, NT)
            pairing = jnp.where(low_rows, state * pltpu.roll(state, LANES - 4, 0), 0.0)
            pairing = jnp.sum(pairing.reshape(SEQ, 8, LANES), axis=0)
            pairing = jnp.concatenate([pairing, jnp.zeros((8, LANES), f32)], axis=0)
            lines = jnp.concatenate([weighted * out, ending * reach, pairing], axis=0)
            sums = sums + mm(jnp.concatenate(high_low(lines), axis=0), gather_matrix(pair))
            whole = scaled_ref[:, cols] + end_w * reach
            head_grad_ref[:, cols] = (g * skip_w + step_w * whole).astype(bf16)
    crossed = crossed[0 : 2 * TOK] + crossed[2 * TOK :]
    sums = sums[0 : 2 * TOK + 16] + sums[2 * TOK + 16 :]
    through, reached = sums[0:TOK], sums[TOK : 2 * TOK]
    paired = jnp.sum(sums[2 * TOK : 2 * TOK + 8], axis=0, keepdims=True)
    own = own_ref[...]
    decay_grad = (
        mm_exact(ones_where(lane >= row), later_ref[...] - step * own + through)
        + mm_exact(ones_where(lane < row), step * reached)
        + jnp.exp(total) * paired
    )
    step_grad = own + reached - triple(rate_ref[...]) * decay_grad
    pre_grad = step_grad * jax.nn.sigmoid(pre)
    pre_grad = jnp.where(lane < 3 * HEADS, pre_grad, 0.0)
    across = across_ref[...]
    bc_grad = mm_exact(across, c_low) + mm_exact(across.T, b_high)
    bc_grad = bc_grad + jnp.where(
        low, pltpu.roll(crossed[TOK:], LANES - 4, 1), pltpu.roll(crossed[0:TOK], 4, 1)
    )
    grads = high_low(jnp.concatenate([bc_grad, pre_grad], axis=1))
    tall, flat = jnp.concatenate(grads, axis=0), jnp.concatenate(grads, axis=1)
    for part in range(10):
        cols = slice(256 * part, 256 * part + 256)
        product = lax.dot_general(tall, weight_ref[cols, :], NT, preferred_element_type=f32)
        input_grad_ref[:, cols] = (product[0:TOK] + product[TOK:]).astype(bf16)
    first_core = core_ref[0] == 0
    lane32 = iota((32, LANES), 1)
    zeros = jnp.zeros((16, LANES), f32)
    for part in range(4):
        cols = slice(640 * part, 640 * part + 640)
        product = lax.dot_general(feat_ref[:, cols], flat, TN, preferred_element_type=f32)
        product = product[:, 0 : 2 * LANES] + product[:, 2 * LANES :]
        for inner in range(8):
            base = ROWS * inner
            dt = product[base : base + 80, LANES:]
            packed = jnp.where(
                lane32 < 40,
                dt[0:32],
                jnp.where(lane32 < 80, dt[32:64], jnp.concatenate([dt[64:80], zeros], axis=0)),
            )
            one = product[base : base + 64, 0:LANES]
            two = jnp.concatenate([product[base + 64 : base + 80, 0:LANES], packed, zeros], axis=0)
            owner = 8 * part + inner
            keep_ref[owner] = jnp.where(first_core, one, two)
            send_ref[owner] = jnp.where(first_core, two, one).astype(bf16)


def finish_kernel(parts_ref, bc_ref, dt_ref):
    one = parts_ref[0].astype(f32)
    two = parts_ref[1].astype(f32)
    for place in range(2, SEQ, 2):
        one = one + parts_ref[place].astype(f32)
        two = two + parts_ref[place + 1].astype(f32)
    scale = 1.0 / math.sqrt(SEQ * DP * TOK)
    bc = jnp.concatenate([one, two[0:16]], axis=0) * scale
    bc_ref[...] = mm_exact(bc, interleave((LANES, LANES), 1))
    packed = two[16:48] * scale
    lane, column = iota((LANES, HEADS), 0), iota((LANES, HEADS), 1)
    for k in range(3):
        rows = min(32, ROWS - 32 * k)
        dt_ref[32 * k : 32 * k + rows, :] = mm_exact(
            packed[0:rows], ones_where(lane == column + 40 * k)
        )


def call(kernel, name, out_shape, scalars, arrays, scratch=(), flops=0, bytes_accessed=0):
    smem = pl.BlockSpec(memory_space=pltpu.SMEM)
    vmem = pl.BlockSpec(memory_space=pltpu.VMEM)
    return pl.pallas_call(
        kernel,
        name=name,
        out_shape=out_shape,
        in_specs=[smem] * len(scalars) + [vmem] * len(arrays),
        out_specs=jax.tree.map(lambda _: vmem, out_shape),
        scratch_shapes=scratch,
        compiler_params=pltpu.CompilerParams(vmem_limit_bytes=40 << 20),
        cost_estimate=pl.CostEstimate(
            flops=flops, bytes_accessed=bytes_accessed, transcendentals=0
        ),
    )(*scalars, *arrays)


def shape(dims, dtype):
    return jax.ShapeDtypeStruct(dims, dtype)


SWAP = [(place, place ^ 1) for place in range(SEQ)]


def body(features, head_inputs, out_grad, bc_weight, dt_weight, dt_bias, decay_rate, skip_gain):
    core = (lax.axis_index("seq") & 1).astype(jnp.int32).reshape(1)
    feats, x, g = features[0], head_inputs[0], out_grad[0]
    bias, rate, skip = dt_bias[None], decay_rate[None], skip_gain[None]
    square = shape((TOK, LANES), f32)
    chunks = shape((DP, HALF, LANES), bf16)

    sent = call(pack_kernel, "pack", chunks, [core], [bc_weight, dt_weight])
    mine = lax.all_to_all(sent, "dp", 0, 0, tiled=True)
    other = lax.ppermute(mine, "seq", SWAP)
    weight, proj, pre, cum, local = call(
        first_kernel,
        "first",
        (shape((WIDE, 2 * LANES), bf16), square, square, square, shape((SEQ, 176, LANES), bf16)),
        [core],
        [mine, other, feats, x, g, bias, rate],
    )
    gathered = lax.all_to_all(local, "seq", 0, 0, tiled=True)
    scaled, across, later, own = call(
        inside_kernel,
        "inside",
        (shape((TOK, WIDE), f32), square, square, square),
        [],
        [proj, pre, cum, x, g],
        scratch=[pltpu.VMEM((LANES, TOK), f32)],
        flops=400_000_000,
        bytes_accessed=4_000_000,
    )
    entering = call(chain_kernel, "chain", shape((SEQ, 160, LANES), bf16), [], [gathered])
    carried = lax.all_to_all(entering, "seq", 0, 0, tiled=True)
    input_grad, head_grad, keep, send = call(
        last_kernel,
        "last",
        (shape((TOK, WIDE), bf16), shape((TOK, WIDE), bf16), shape((DP, HALF, LANES), f32), chunks),
        [core],
        [carried, weight, proj, pre, cum, scaled, across, later, own, feats, x, g, rate, skip],
    )
    paired = (keep + lax.ppermute(send, "seq", SWAP).astype(f32)).astype(bf16)
    owned = lax.all_to_all(paired, "dp", 0, 0, tiled=True)
    owned = jnp.sum(owned.astype(f32), axis=0)
    parts = lax.all_gather(owned, "seq")
    bc_grad, dt_grad = call(
        finish_kernel, "finish", (shape((ROWS, LANES), f32), shape((ROWS, HEADS), f32)), [], [parts]
    )
    return input_grad[None], head_grad[None], bc_grad, dt_grad


def solution(mesh):
    in_specs = (
        P("dp", "seq", None),
        P("dp", "seq", None),
        P("dp", "seq", None),
        P("dp", None),
        P("dp", None),
        P(),
        P(),
        P(),
    )
    out_specs = (P("dp", "seq", None), P("dp", "seq", None), P("dp", None), P("dp", None))
    return jax.shard_map(body, mesh=mesh, in_specs=in_specs, out_specs=out_specs, check_vma=False)
```

time: 585 us -> 150 us (0.26)
  the two profiles are of different devices: /device:TPU:16 before, /device:TPU:9 now
where the time goes in v1:
time: 150 us
  blocking collectives  96.8 us (65%)
  Pallas kernels  18.7 us (12%)
  waiting for transfers between devices  15.6 us (10%)
  starting transfers between devices  10.6 us (7%)
  local copies, waits for them, and re-layouts  7.12 us (5%)
    all_to_all x1, blocking collectives, body(): gathered = lax.all_to_all(local, 'seq', 0, 0, tiled=True)  32 us
    all_to_all x1, blocking collectives, body(): mine = lax.all_to_all(sent, 'dp', 0, 0, tiled=True)  25.4 us
    all_to_all x1, blocking collectives, body(): owned = lax.all_to_all(paired, 'dp', 0, 0, tiled=True)  21 us
    pallas_call x6, Pallas kernels, call(): pl.pallas_call(kernel, name=name, out_shape=out_shape, in_specs=[smem] *...  18.7 us
    all_gather x1, blocking collectives, body(): parts = lax.all_gather(owned, 'seq')  18.4 us
    all_to_all x1, waiting for transfers between devices, body(): carried = lax.all_to_all(entering, 'seq', 0, 0, tiled=True)  12.3 us
    unnamed x26, local copies, waits for them, and re-layouts  7.12 us
    ppermute x1, starting transfers between devices, body(): other = lax.ppermute(mine, 'seq', SWAP)  4.74 us
  transfers between devices with their start and end apart: 3, of which 3 were waited for; matrix products, arithmetic and copies ran while one was open for 0% of the time, Pallas kernels for 3%

profile of v1, /device:TPU:9, one launch (start us, length us, event | category | flops | bytes accessed | tf_op | source)
XLA Modules:
  0.0 149.8 jit_solution(3399988469411093269)
XLA Ops:
  0.7 0.9 copy.12.dt_ref
  1.6 0.7 copy-done.8
  2.3 0.2 pack.1
  2.5 25.4 %all_to_all.20.mine_ref = bf16[32,64,128]{2,1,0:T(8,128)(2,1)S(1)} all-to-all(bf16[32,64,128]{2,1,0:T(8,128)(2,1)S(1)} %pack.1), channel_id=1, replica_groups=mesh['dp'=32,'seq'=16] {'dp'}, dimensions={0} | all-to-all | bytes 1048576 | tf_op jit(solution)/shard_map/all_to_all | solution.py:398
  27.9 4.7 %collective-permute-start = (bf16[32,64,128]{2,1,0:T(8,128)(2,1)S(1)}, bf16[32,64,128]{2,1,0:T(8,128)(2,1)S(1)}, u32[]{:S(2)}, u32[]{:S(2)}) collective-permute-start(bf16[32,64,128]{2,1,0:T(8,128)(2,1)S(1)} %all_to_all.20.mine_ref), channel_id=1, source_target_pairs={{0,1},{1,0},{2,3},{3,2},{4,5},{5,4},{6,7},{7,6},{8,9},{9,8},{10,11... | collective-permute-start | bytes 1572872 | tf_op jit(solution)/shard_map/ppermute | solution.py:399
  32.7 1.5 %collective-permute-done.other_ref = bf16[32,64,128]{2,1,0:T(8,128)(2,1)S(1)} collective-permute-done((bf16[32,64,128]{2,1,0:T(8,128)(2,1)S(1)}, bf16[32,64,128]{2,1,0:T(8,128)(2,1)S(1)}, u32[]{:S(2)}, u32[]{:S(2)}) %collective-permute-start) | collective-permute-done | bytes 524320 | tf_op jit(solution)/shard_map/ppermute | solution.py:399
  34.2 1.1 copy-done.2
  35.3 3.9 %first.1 = (bf16[2560,256]{1,0:T(8,128)(2,1)S(1)}, f32[128,128]{1,0:T(8,128)S(1)}, f32[128,128]{1,0:T(8,128)S(1)}, f32[128,128]{1,0:T(8,128)S(1)}, bf16[16,176,128]{2,1,0:T(8,128)(2,1)S(1)}) custom-call(s32[1]{0:T(128)} %bitcast.core_ref, bf16[32,64,128]{2,1,0:T(8,128)(2,1)S(1)} %all_to_all.20.mine_ref, ...), custom_call_target="tpu_custom_call" | custom-call | tf_op jit(solution)/shard_map/first/pallas_call | solution.py:369
  39.2 32.0 %all_to_all.21.state_ref = bf16[16,176,128]{2,1,0:T(8,128)(2,1)S(1)} all-to-all(bf16[16,176,128]{2,1,0:T(8,128)(2,1)S(1)} %get-tuple-element.19), channel_id=1, replica_groups=mesh['dp'=32,'seq'=16] {'seq'}, dimensions={0} | all-to-all | bytes 1441792 | tf_op jit(solution)/shard_map/all_to_all | solution.py:407
  71.3 1.4 chain.1
  72.7 3.8 %all-to-all-start.2 = ((bf16[16,160,128]{2,1,0:T(8,128)(2,1)}), bf16[16,160,128]{2,1,0:T(8,128)(2,1)S(1)}, u32[]{:S(2)}, u32[]{:S(2)}) async-start(bf16[16,160,128]{2,1,0:T(8,128)(2,1)} %chain.1), calls=%async_computation.2 | async-start | bytes 1310720 | tf_op jit(solution)/shard_map/all_to_all | solution.py:419
  76.5 4.6 %inside.1 = (f32[128,2560]{1,0:T(8,128)S(1)}, f32[128,128]{1,0:T(8,128)S(1)}, f32[128,128]{1,0:T(8,128)S(1)}, f32[128,128]{1,0:T(8,128)S(1)}) custom-call(f32[128,128]{1,0:T(8,128)S(1)} %get-tuple-element.21.proj_ref, f32[128,128]{1,0:T(8,128)S(1)} %get-tuple-element.22.pre_ref, f32[128,128]{1,0:T(8,128)S(1)} %get-tuple-element.23.cum_ref, ...), custom_call_target="tpu_custom_call" | custom-call | flops 400000000 | bytes 4000000 | tf_op jit(solution)/shard_map/inside/pallas_call | solution.py:369
  81.1 1.1 copy-done.6
  82.2 12.3 %all-to-all-done.2.carried_ref = bf16[16,160,128]{2,1,0:T(8,128)(2,1)S(1)} async-done(((bf16[16,160,128]{2,1,0:T(8,128)(2,1)}), bf16[16,160,128]{2,1,0:T(8,128)(2,1)S(1)}, u32[]{:S(2)}, u32[]{:S(2)}) %all-to-all-start.2) | async-done | bytes 655392 | tf_op jit(solution)/shard_map/all_to_all | solution.py:419
  94.5 1.3 copy-done.5
  95.8 1.3 copy-done.7
  97.1 7.7 %last.1 = (bf16[128,2560]{1,0:T(8,128)(2,1)}, bf16[128,2560]{1,0:T(8,128)(2,1)}, f32[32,64,128]{2,1,0:T(8,128)S(1)}, bf16[32,64,128]{2,1,0:T(8,128)(2,1)S(1)}) custom-call(s32[1]{0:T(128)} %bitcast.core_ref, bf16[16,160,128]{2,1,0:T(8,128)(2,1)S(1)} %all-to-all-done.2.carried_ref, bf16[2560,256]{1,0:T(8,128)(2,1)S(1)} %copy-done.5, ...), custom_call_target="tpu_custom_call" | custom-call | tf_op jit(solution)/shard_map/last/pallas_call | solution.py:369
  104.8 2.0 %collective-permute-start.1 = (bf16[32,64,128]{2,1,0:T(8,128)(2,1)S(1)}, bf16[32,64,128]{2,1,0:T(8,128)(2,1)S(1)}, u32[]{:S(2)}, u32[]{:S(2)}) collective-permute-start(bf16[32,64,128]{2,1,0:T(8,128)(2,1)S(1)} %get-tuple-element.31), channel_id=1, source_target_pairs={{0,1},{1,0},{2,3},{3,2},{4,5},{5,4},{6,7},{7,6},{8,9},{9,8},{10,11... | collective-permute-start | bytes 1572872 | tf_op jit(solution)/shard_map/ppermute | solution.py:427
  106.9 1.8 %collective-permute-done.1 = bf16[32,64,128]{2,1,0:T(8,128)(2,1)S(1)} collective-permute-done((bf16[32,64,128]{2,1,0:T(8,128)(2,1)S(1)}, bf16[32,64,128]{2,1,0:T(8,128)(2,1)S(1)}, u32[]{:S(2)}, u32[]{:S(2)}) %collective-permute-start.1) | collective-permute-done | bytes 524320 | tf_op jit(solution)/shard_map/ppermute | solution.py:427
  108.6 0.2 add_convert_fusion
  108.8 21.0 %all_to_all.22 = bf16[32,64,128]{2,1,0:T(8,128)(2,1)S(1)} all-to-all(bf16[32,64,128]{2,1,0:T(8,128)(2,1)S(1)} %add_convert_fusion), channel_id=1, replica_groups=mesh['dp'=32,'seq'=16] {'dp'}, dimensions={0} | all-to-all | bytes 1048576 | tf_op jit(solution)/shard_map/all_to_all | solution.py:428
  129.9 18.4 %all-gather = f32[1024,128]{1,0:T(8,128)S(1)} all-gather(f32[64,128]{1,0:T(8,128)S(1)} %convert_reduce_fusion), channel_id=2, replica_groups=mesh['dp'=32,'seq'=16] {'seq'}, dimensions={0}, use_global_device_ids=true | all-gather | bytes 557056 | tf_op jit(solution)/shard_map/all_gather | solution.py:430
  148.2 0.9 finish.1
  149.1 0.7 copy.13
  (20 shorter events, 0.1 us)
Async XLA Ops:
  0.6 33.5 %copy-start.1 = (bf16[1,128,2560]{2,1,0:T(8,128)(2,1)S(1)}, bf16[1,128,2560]{2,1,0:T(8,128)(2,1)}, u32[]{:S(2)}) copy-start(bf16[1,128,2560]{2,1,0:T(8,128)(2,1)} %param.10) | copy-start | bytes 1966084
  0.6 33.5 %copy-start = (bf16[1,128,2560]{2,1,0:T(8,128)(2,1)S(1)}, bf16[1,128,2560]{2,1,0:T(8,128)(2,1)}, u32[]{:S(2)}) copy-start(bf16[1,128,2560]{2,1,0:T(8,128)(2,1)} %param.9) | copy-start | bytes 1966084
  1.6 0.7 copy-start.8
  2.3 31.9 %copy-start.9 = (f32[40]{0:T(128)S(1)}, f32[40]{0:T(128)}, u32[]{:S(2)}) copy-start(f32[40]{0:T(128)} %param.14) | copy-start | bytes 484
  2.3 31.9 %copy-start.10 = (f32[40]{0:T(128)S(1)}, f32[40]{0:T(128)}, u32[]{:S(2)}) copy-start(f32[40]{0:T(128)} %param.13) | copy-start | bytes 484
  27.9 6.3 %collective-permute-start = (bf16[32,64,128]{2,1,0:T(8,128)(2,1)S(1)}, bf16[32,64,128]{2,1,0:T(8,128)(2,1)S(1)}, u32[]{:S(2)}, u32[]{:S(2)}) collective-permute-start(bf16[32,64,128]{2,1,0:T(8,128)(2,1)S(1)} %all_to_all.20.mine_ref), channel_id=1, source_target_pairs={{0,1},{1,0},{2,3},{3,2},{4,5},{5,4},{6,7},{7,6},{8,9},{9,8},{10,11... | collective-permute-start | bytes 1572872 | tf_op jit(solution)/shard_map/ppermute | solution.py:399
  34.2 1.1 copy-start.2
  39.2 32.0 %copy-start.4 = (bf16[2560,256]{1,0:T(8,128)(2,1)}, bf16[2560,256]{1,0:T(8,128)(2,1)S(1)}, u32[]{:S(2)}) copy-start(bf16[2560,256]{1,0:T(8,128)(2,1)S(1)} %get-tuple-element.20.weight_ref) | copy-start | bytes 3932164
  72.7 21.8 %copy-start.3 = (bf16[1,128,2560]{2,1,0:T(8,128)(2,1)S(1)}, bf16[1,128,2560]{2,1,0:T(8,128)(2,1)}, u32[]{:S(2)}) copy-start(bf16[1,128,2560]{2,1,0:T(8,128)(2,1)} %param.8) | copy-start | bytes 1966084
  72.7 21.8 %copy-start.11 = (f32[40]{0:T(128)S(1)}, f32[40]{0:T(128)}, u32[]{:S(2)}) copy-start(f32[40]{0:T(128)} %param.15) | copy-start | bytes 484
  72.7 21.8 %all-to-all-start.2 = ((bf16[16,160,128]{2,1,0:T(8,128)(2,1)}), bf16[16,160,128]{2,1,0:T(8,128)(2,1)S(1)}, u32[]{:S(2)}, u32[]{:S(2)}) async-start(bf16[16,160,128]{2,1,0:T(8,128)(2,1)} %chain.1), calls=%async_computation.2 | async-start | bytes 1310720 | tf_op jit(solution)/shard_map/all_to_all | solution.py:419
  81.1 1.1 copy-start.6
  94.5 1.3 copy-start.5
  95.8 1.3 copy-start.7
  104.8 3.8 %collective-permute-start.1 = (bf16[32,64,128]{2,1,0:T(8,128)(2,1)S(1)}, bf16[32,64,128]{2,1,0:T(8,128)(2,1)S(1)}, u32[]{:S(2)}, u32[]{:S(2)}) collective-permute-start(bf16[32,64,128]{2,1,0:T(8,128)(2,1)S(1)} %get-tuple-element.31), channel_id=1, source_target_pairs={{0,1},{1,0},{2,3},{3,2},{4,5},{5,4},{6,7},{7,6},{8,9},{9,8},{10,11... | collective-permute-start | bytes 1572872 | tf_op jit(solution)/shard_map/ppermute | solution.py:427

commit v2 on v1

--- a/solution.py
+++ b/solution.py
@@ -1,4 +1,5 @@
 import math
+from functools import partial
 
 import jax
 import jax.numpy as jnp
@@ -17,7 +18,8 @@
 ROWS = 80
 DP = 32
 SEQ = 16
-HALF = 64
+HALF = 56
+REST = 24
 LANES = 128
 
 NN = (((1,), (0,)), ((), ()))
@@ -84,15 +86,19 @@
 def pack_kernel(core_ref, bc_ref, dt_ref, out_ref):
     bc = mm(bc_ref[...], interleave((LANES, LANES), 0))
     row, lane = iota((HEADS, LANES), 0), iota((HEADS, LANES), 1)
-    dt = dt_ref[...]
-    packed = mm(dt[0:32], ones_where(lane == row)) + mm(dt[32:64], ones_where(lane == row + 40))
-    last = mm(dt[64:80], ones_where(lane == row + 80))
-    zeros = jnp.zeros((16, LANES), f32)
-    packed = packed + jnp.concatenate([last, zeros], axis=0)
-    second = jnp.concatenate([bc[64:80], packed, zeros], axis=0)
-    value = jnp.where(core_ref[0] == 0, bc[0:64], second).astype(bf16)
+    dt = [mm(dt_ref[...], ones_where(lane == row + 40 * k), TN) for k in range(3)]
+    last = jnp.concatenate([dt[2][64:80], jnp.zeros((16, LANES), f32)], axis=0)
+    packed = dt[0][0:32] + dt[1][32:64] + last
+    second = jnp.concatenate([bc[HALF:ROWS], packed], axis=0)
+    value = jnp.where(core_ref[0] == 0, bc[0:HALF], second).astype(bf16)
     for owner in range(DP):
         out_ref[owner] = value
+
+
+def turn_kernel(feat_ref, out_ref):
+    for part in range(PAIRS):
+        rows = slice(LANES * part, LANES * part + LANES)
+        out_ref[rows, :] = feat_ref[:, rows].T
 
 
 def first_kernel(
@@ -107,9 +113,9 @@
     def assemble(one_ref, two_ref):
         for owner in range(DP):
             base = ROWS * owner
-            weight_ref[base : base + 64, 0:LANES] = one_ref[owner]
-            weight_ref[base + 64 : base + 80, 0:LANES] = two_ref[owner, 0:16, :]
-            low, high = two_ref[owner, 16:32, :], two_ref[owner, 32:48, :]
+            weight_ref[base : base + HALF, 0:LANES] = one_ref[owner]
+            weight_ref[base + HALF : base + ROWS, 0:LANES] = two_ref[owner, 0:REST, :]
+            low, high = two_ref[owner, 24:40, :], two_ref[owner, 40:56, :]
             weight_ref[base : base + 16, LANES:] = low * group[0]
             weight_ref[base + 16 : base + 32, LANES:] = high * group[0]
             weight_ref[base + 32 : base + 48, LANES:] = low * group[1]
@@ -158,16 +164,17 @@
     for two in range(PAIRS // 2):
         value = jnp.concatenate([block(2 * two), block(2 * two + 1)], axis=1)
         state_ref[:, 16 * two : 16 * two + 16, :] = value.astype(bf16)
-    decay = split(jnp.broadcast_to(total, (16, LANES)))
+    decay = split(jnp.broadcast_to(total, (8, LANES)))
     for owner in range(SEQ):
-        state_ref[owner, 160:176, :] = decay
-
-
-def chain_kernel(state_ref, out_ref):
+        state_ref[owner, 160:168, :] = decay
+
+
+def chain_kernel(state_ref, after_ref, out_ref):
     row16 = iota((16, LANES), 0)
     logs = jnp.zeros((16, LANES), f32)
     for place in range(SEQ):
-        logs = logs + jnp.where(row16 == place, state_ref[place, 160:176, :].astype(f32), 0.0)
+        line = state_ref[place, 160:168, :].astype(f32)
+        logs = logs + jnp.where(row16 == place, jnp.concatenate([line, line], axis=0), 0.0)
     logs = logs.astype(bf16)
     forward = (row16 & 7) < 4
     for two in range(PAIRS // 2):
@@ -202,9 +209,9 @@
     return jnp.maximum(pre, 0.0) + jnp.log1p(jnp.exp(-jnp.abs(pre)))
 
 
-def inside_kernel(
-    proj_ref, pre_ref, cum_ref, x_ref, g_ref, scaled_ref, across_ref, later_ref, own_ref, rows_ref
-):
+def inside_kernel(first_pair, start, *refs):
+    proj_ref, pre_ref, cum_ref, x_ref, g_ref = refs[:5]
+    scaled_ref, across_ref, own_ref, rows_ref = refs[-4:]
     proj, cum = proj_ref[...], cum_ref[...]
     step = softplus(pre_ref[...])
     row, lane = iota((LANES, LANES), 0), iota((LANES, LANES), 1)
@@ -215,12 +222,16 @@
     causal = lane >= row
     cum_turned = cum.T
     lane_head = head_of_lane(lane)
-    across = jnp.zeros((TOK, TOK), f32)
-    own = jnp.zeros((TOK, LANES), f32)
+    if start:
+        across = jnp.zeros((TOK, TOK), f32)
+        own = jnp.zeros((TOK, LANES), f32)
+        rows_ref[...] = jnp.zeros_like(rows_ref)
+    else:
+        across, own = refs[5][...], refs[6][...]
+        rows_ref[...] = refs[7][...]
     first_half = ones_where(lane < 64, bf16)
     second_half = ones_where(lane >= 64, bf16)
-    rows_ref[...] = jnp.zeros_like(rows_ref)
-    for pair in range(PAIRS):
+    for pair in range(first_pair, first_pair + PAIRS // 2):
         cols = slice(LANES * pair, LANES * pair + LANES)
         x, g = x_ref[:, cols], g_ref[:, cols]
         mixed, parts = [], []
@@ -238,20 +249,19 @@
             rows_ref[head : head + 1, :] = jnp.sum(product * step_col, axis=0, keepdims=True)
             mixed.append((meet * weight).astype(bf16))
             parts.append(g_half)
-        scaled_ref[:, cols] = lax.dot_general(
+        here = slice(LANES * (pair - first_pair), LANES * (pair - first_pair) + LANES)
+        scaled_ref[:, here] = lax.dot_general(
             jnp.concatenate(mixed, axis=1), jnp.concatenate(parts, axis=0), NN,
             preferred_element_type=f32,
         )
     across_ref[...] = across
     own_ref[...] = own
-    place = ones_where((row == lane_head) & (row < HEADS))
-    later_ref[...] = mm_exact(rows_ref[...].T, place)
 
 
 def last_kernel(
-    core_ref, carried_ref, weight_ref, proj_ref, pre_ref, cum_ref, scaled_ref, across_ref,
-    later_ref, own_ref, feat_ref, x_ref, g_ref, rate_ref, skip_ref,
-    input_grad_ref, head_grad_ref, keep_ref, send_ref,
+    core_ref, carried_ref, proj_ref, pre_ref, cum_ref, left_ref, right_ref, across_ref,
+    own_ref, rows_ref, turned_ref, x_ref, g_ref, rate_ref, skip_ref,
+    grads_ref, head_grad_ref, keep_ref, send_ref,
 ):
     proj, pre, cum = proj_ref[...], pre_ref[...], cum_ref[...]
     step = softplus(pre)
@@ -297,15 +307,19 @@
             pairing = jnp.concatenate([pairing, jnp.zeros((8, LANES), f32)], axis=0)
             lines = jnp.concatenate([weighted * out, ending * reach, pairing], axis=0)
             sums = sums + mm(jnp.concatenate(high_low(lines), axis=0), gather_matrix(pair))
-            whole = scaled_ref[:, cols] + end_w * reach
+            half_ref = left_ref if two < 5 else right_ref
+            first_lane = LANES * (pair % 10)
+            whole = half_ref[:, first_lane : first_lane + LANES] + end_w * reach
             head_grad_ref[:, cols] = (g * skip_w + step_w * whole).astype(bf16)
     crossed = crossed[0 : 2 * TOK] + crossed[2 * TOK :]
     sums = sums[0 : 2 * TOK + 16] + sums[2 * TOK + 16 :]
     through, reached = sums[0:TOK], sums[TOK : 2 * TOK]
     paired = jnp.sum(sums[2 * TOK : 2 * TOK + 8], axis=0, keepdims=True)
     own = own_ref[...]
+    lane_head = head_of_lane(lane)
+    later = mm_exact(rows_ref[...].T, ones_where((row == lane_head) & (row < HEADS)))
     decay_grad = (
-        mm_exact(ones_where(lane >= row), later_ref[...] - step * own + through)
+        mm_exact(ones_where(lane >= row), later - step * own + through)
         + mm_exact(ones_where(lane < row), step * reached)
         + jnp.exp(total) * paired
     )
@@ -319,30 +333,35 @@
     )
     grads = high_low(jnp.concatenate([bc_grad, pre_grad], axis=1))
     tall, flat = jnp.concatenate(grads, axis=0), jnp.concatenate(grads, axis=1)
-    for part in range(10):
-        cols = slice(256 * part, 256 * part + 256)
-        product = lax.dot_general(tall, weight_ref[cols, :], NT, preferred_element_type=f32)
-        input_grad_ref[:, cols] = (product[0:TOK] + product[TOK:]).astype(bf16)
+    grads_ref[...] = tall
     first_core = core_ref[0] == 0
     lane32 = iota((32, LANES), 1)
     zeros = jnp.zeros((16, LANES), f32)
     for part in range(4):
-        cols = slice(640 * part, 640 * part + 640)
-        product = lax.dot_general(feat_ref[:, cols], flat, TN, preferred_element_type=f32)
+        rows = slice(640 * part, 640 * part + 640)
+        product = lax.dot_general(turned_ref[rows, :], flat, NN, preferred_element_type=f32)
         product = product[:, 0 : 2 * LANES] + product[:, 2 * LANES :]
         for inner in range(8):
             base = ROWS * inner
-            dt = product[base : base + 80, LANES:]
+            dt = product[base : base + ROWS, LANES:]
             packed = jnp.where(
                 lane32 < 40,
                 dt[0:32],
                 jnp.where(lane32 < 80, dt[32:64], jnp.concatenate([dt[64:80], zeros], axis=0)),
             )
-            one = product[base : base + 64, 0:LANES]
-            two = jnp.concatenate([product[base + 64 : base + 80, 0:LANES], packed, zeros], axis=0)
+            one = product[base : base + HALF, 0:LANES]
+            two = jnp.concatenate([product[base + HALF : base + ROWS, 0:LANES], packed], axis=0)
             owner = 8 * part + inner
             keep_ref[owner] = jnp.where(first_core, one, two)
             send_ref[owner] = jnp.where(first_core, two, one).astype(bf16)
+
+
+def back_kernel(grads_ref, weight_ref, input_grad_ref):
+    tall = grads_ref[...]
+    for part in range(10):
+        cols = slice(256 * part, 256 * part + 256)
+        product = lax.dot_general(tall, weight_ref[cols, :], NT, preferred_element_type=f32)
+        input_grad_ref[:, cols] = (product[0:TOK] + product[TOK:]).astype(bf16)
 
 
 def finish_kernel(parts_ref, bc_ref, dt_ref):
@@ -352,14 +371,14 @@
         one = one + parts_ref[place].astype(f32)
         two = two + parts_ref[place + 1].astype(f32)
     scale = 1.0 / math.sqrt(SEQ * DP * TOK)
-    bc = jnp.concatenate([one, two[0:16]], axis=0) * scale
+    bc = jnp.concatenate([one, two[0:REST]], axis=0) * scale
     bc_ref[...] = mm_exact(bc, interleave((LANES, LANES), 1))
-    packed = two[16:48] * scale
-    lane, column = iota((LANES, HEADS), 0), iota((LANES, HEADS), 1)
+    packed = two[REST:HALF] * scale
+    head, lane = iota((HEADS, LANES), 0), iota((HEADS, LANES), 1)
     for k in range(3):
         rows = min(32, ROWS - 32 * k)
-        dt_ref[32 * k : 32 * k + rows, :] = mm_exact(
-            packed[0:rows], ones_where(lane == column + 40 * k)
+        dt_ref[:, 32 * k : 32 * k + rows] = mm_exact(
+            ones_where(lane == head + 40 * k), packed[0:rows], NT
         )
 
 
@@ -373,7 +392,7 @@
         in_specs=[smem] * len(scalars) + [vmem] * len(arrays),
         out_specs=jax.tree.map(lambda _: vmem, out_shape),
         scratch_shapes=scratch,
-        compiler_params=pltpu.CompilerParams(vmem_limit_bytes=40 << 20),
+        compiler_params=pltpu.CompilerParams(vmem_limit_bytes=20 << 20),
         cost_estimate=pl.CostEstimate(
             flops=flops, bytes_accessed=bytes_accessed, transcendentals=0
         ),
@@ -394,44 +413,55 @@
     square = shape((TOK, LANES), f32)
     chunks = shape((DP, HALF, LANES), bf16)
 
-    sent = call(pack_kernel, "pack", chunks, [core], [bc_weight, dt_weight])
+    sent = call(pack_kernel, "pack", chunks, [core], [bc_weight, dt_weight.T])
     mine = lax.all_to_all(sent, "dp", 0, 0, tiled=True)
+    turned = call(turn_kernel, "turn", shape((WIDE, TOK), bf16), [], [feats], bytes_accessed=2_000_000)
     other = lax.ppermute(mine, "seq", SWAP)
     weight, proj, pre, cum, local = call(
         first_kernel,
         "first",
-        (shape((WIDE, 2 * LANES), bf16), square, square, square, shape((SEQ, 176, LANES), bf16)),
+        (shape((WIDE, 2 * LANES), bf16), square, square, square, shape((SEQ, 168, LANES), bf16)),
         [core],
         [mine, other, feats, x, g, bias, rate],
     )
     gathered = lax.all_to_all(local, "seq", 0, 0, tiled=True)
-    scaled, across, later, own = call(
-        inside_kernel,
-        "inside",
-        (shape((TOK, WIDE), f32), square, square, square),
-        [],
-        [proj, pre, cum, x, g],
-        scratch=[pltpu.VMEM((LANES, TOK), f32)],
-        flops=400_000_000,
-        bytes_accessed=4_000_000,
-    )
-    entering = call(chain_kernel, "chain", shape((SEQ, 160, LANES), bf16), [], [gathered])
+    half = (shape((TOK, WIDE // 2), f32), square, square, square)
+    cost = dict(flops=200_000_000, bytes_accessed=3_000_000)
+    left, across, own, rows = call(
+        partial(inside_kernel, 0, True), "inside_left", half, [], [proj, pre, cum, x, g], **cost
+    )
+    entering = call(
+        chain_kernel, "chain", shape((SEQ, 160, LANES), bf16), [], [gathered, across[0:8]]
+    )
     carried = lax.all_to_all(entering, "seq", 0, 0, tiled=True)
-    input_grad, head_grad, keep, send = call(
+    right, across, own, rows = call(
+        partial(inside_kernel, PAIRS // 2, False), "inside_right", half, [],
+        [proj, pre, cum, x, g, across, own, rows], **cost,
+    )
+    grads, head_grad, keep, send = call(
         last_kernel,
         "last",
-        (shape((TOK, WIDE), bf16), shape((TOK, WIDE), bf16), shape((DP, HALF, LANES), f32), chunks),
+        (
+            shape((2 * TOK, 2 * LANES), bf16),
+            shape((TOK, WIDE), bf16),
+            shape((DP, HALF, LANES), f32),
+            chunks,
+        ),
         [core],
-        [carried, weight, proj, pre, cum, scaled, across, later, own, feats, x, g, rate, skip],
+        [carried, proj, pre, cum, left, right, across, own, rows, turned, x, g, rate, skip],
     )
     paired = (keep + lax.ppermute(send, "seq", SWAP).astype(f32)).astype(bf16)
     owned = lax.all_to_all(paired, "dp", 0, 0, tiled=True)
+    input_grad = call(
+        back_kernel, "back", shape((TOK, WIDE), bf16), [], [grads, weight],
+        flops=340_000_000, bytes_accessed=3_000_000,
+    )
     owned = jnp.sum(owned.astype(f32), axis=0)
     parts = lax.all_gather(owned, "seq")
     bc_grad, dt_grad = call(
-        finish_kernel, "finish", (shape((ROWS, LANES), f32), shape((ROWS, HEADS), f32)), [], [parts]
-    )
-    return input_grad[None], head_grad[None], bc_grad, dt_grad
+        finish_kernel, "finish", (shape((ROWS, LANES), f32), shape((HEADS, ROWS), f32)), [], [parts]
+    )
+    return input_grad[None], head_grad[None], bc_grad, dt_grad.T
 
 
 def solution(mesh):

time: 150 us -> 151 us (level)
  blocking collectives: 96.8 us -> 41.7 us
  waiting for transfers between devices: 15.6 us -> 47.6 us
  starting transfers between devices: 10.6 us -> 25.2 us
  local copies, waits for them, and re-layouts: 7.12 us -> 12.7 us
  Pallas kernels: 18.7 us -> 20.8 us
    all_to_all x2 -> x0, blocking collectives: 53 us -> none  [the longest x1 32 us: body(): gathered = lax.all_to_all(local, 'seq', 0, 0, tiled=True)]
    all_to_all x0 -> x2, waiting for transfers between devices: none -> 30.9 us  [the longest x1 16.9 us: body(): gathered = lax.all_to_all(local, 'seq', 0, 0, tiled=True)]
    all_to_all x0 -> x2, starting transfers between devices: none -> 15 us  [the longest x1 10.7 us: body(): gathered = lax.all_to_all(local, 'seq', 0, 0, tiled=True)]
    unnamed x26 -> x54, local copies, waits for them, and re-layouts: 7.12 us -> 12.7 us
    pallas_call x6 -> x9, Pallas kernels: 18.7 us -> 20.8 us  [call(): pl.pallas_call(kernel, name=name, out_shape=out_shape, in_specs=[smem] *...]
  transfers between devices with their start and end apart: 3 -> 5, of which waited for: 3 -> 5; matrix products, arithmetic and copies ran while one was open for 0% -> 0% of each run, Pallas kernels for 3% -> 4%
where the time goes in v2:
time: 151 us; the launch traced here: 150 us
  waiting for transfers between devices  47.6 us (32%)
  blocking collectives  41.7 us (28%)
  starting transfers between devices  25.2 us (17%)
  Pallas kernels  20.8 us (14%)
  local copies, waits for them, and re-layouts  12.7 us (8%)
    all_to_all x1, blocking collectives, body(): mine = lax.all_to_all(sent, 'dp', 0, 0, tiled=True)  24.1 us
    pallas_call x9, Pallas kernels, call(): pl.pallas_call(kernel, name=name, out_shape=out_shape, in_specs=[smem] *...  20.8 us
    all_gather x1, blocking collectives, body(): parts = lax.all_gather(owned, 'seq')  17.6 us
    all_to_all x1, waiting for transfers between devices, body(): gathered = lax.all_to_all(local, 'seq', 0, 0, tiled=True)  16.9 us
    all_to_all x1, waiting for transfers between devices, body(): owned = lax.all_to_all(paired, 'dp', 0, 0, tiled=True)  13.9 us
    all_to_all x1, waiting for transfers between devices, body(): carried = lax.all_to_all(entering, 'seq', 0, 0, tiled=True)  13.6 us
    unnamed x54, local copies, waits for them, and re-layouts  12.7 us
    all_to_all x1, starting transfers between devices, body(): gathered = lax.all_to_all(local, 'seq', 0, 0, tiled=True)  10.7 us
  transfers between devices with their start and end apart: 5, of which 5 were waited for; matrix products, arithmetic and copies ran while one was open for 0% of the time, Pallas kernels for 4%

profile of v2, /device:TPU:9, one launch (start us, length us, event | category | flops | bytes accessed | tf_op | source)
XLA Modules:
  0.0 149.8 jit_solution(2939211489622465985)
XLA Ops:
  2.4 24.1 %all_to_all.20.mine_ref = bf16[32,56,128]{2,1,0:T(8,128)(2,1)S(1)} all-to-all(bf16[32,56,128]{2,1,0:T(8,128)(2,1)S(1)} %pack.1), channel_id=1, replica_groups=mesh['dp'=32,'seq'=16] {'dp'}, dimensions={0} | all-to-all | bytes 917504 | tf_op jit(solution)/shard_map/all_to_all | solution.py:417
  26.6 4.6 %collective-permute-start = (bf16[32,56,128]{2,1,0:T(8,128)(2,1)S(1)}, bf16[32,56,128]{2,1,0:T(8,128)(2,1)S(1)}, u32[]{:S(2)}, u32[]{:S(2)}) collective-permute-start(bf16[32,56,128]{2,1,0:T(8,128)(2,1)S(1)} %all_to_all.20.mine_ref), channel_id=1, source_target_pairs={{0,1},{1,0},{2,3},{3,2},{4,5},{5,4},{6,7},{7,6},{8,9},{9,8},{10,11... | collective-permute-start | bytes 1376264 | tf_op jit(solution)/shard_map/ppermute | solution.py:419
  31.2 1.4 collective-permute-done.other_ref
  32.6 1.1 copy-done.2
  33.7 4.8 %first.1 = (bf16[2560,256]{1,0:T(8,128)(2,1)S(1)}, f32[128,128]{1,0:T(8,128)S(1)}, f32[128,128]{1,0:T(8,128)S(1)}, f32[128,128]{1,0:T(8,128)S(1)}, bf16[16,168,128]{2,1,0:T(8,128)(2,1)}) custom-call(s32[1]{0:T(128)} %bitcast.core_ref, bf16[32,56,128]{2,1,0:T(8,128)(2,1)S(1)} %all_to_all.20.mine_ref, bf16[32,56,128]{2,1,0:T(8,128)(2,1)S(1)} %collective-permute-done.other_ref, ...), custom_call_target="tpu_custom_call" | custom-call | tf_op jit(solution)/shard_map/first/pallas_call | solution.py:388
  38.5 1.1 copy-done.4
  39.6 10.7 %all-to-all-start.1 = ((bf16[16,168,128]{2,1,0:T(8,128)(2,1)}), bf16[16,168,128]{2,1,0:T(8,128)(2,1)S(1)}, u32[]{:S(2)}, u32[]{:S(2)}) async-start(bf16[16,168,128]{2,1,0:T(8,128)(2,1)} %get-tuple-element.23), calls=%async_computation.1 | async-start | bytes 1376256 | tf_op jit(solution)/shard_map/all_to_all | solution.py:427
  50.3 2.3 %inside_left.1 = (f32[128,1280]{1,0:T(8,128)S(1)}, f32[128,128]{1,0:T(8,128)S(1)}, f32[128,128]{1,0:T(8,128)S(1)}, f32[128,128]{1,0:T(8,128)S(1)}) custom-call(f32[128,128]{1,0:T(8,128)S(1)} %get-tuple-element.24.refs_0_.proj_ref, f32[128,128]{1,0:T(8,128)S(1)} %get-tuple-element.25.refs_1_.pre_ref, f32[128,128]{1,0:T(8,128)S(1)} %get-tuple-element.26.refs_2_.cum_ref, ...), custom_call_target="tpu_custom_call" | custom-call | flops 200000000 | bytes 3000000 | tf_op jit(solution)/shard_map/inside_left/pallas_call | solution.py:388
  54.0 16.9 %all-to-all-done.1.state_ref = bf16[16,168,128]{2,1,0:T(8,128)(2,1)S(1)} async-done(((bf16[16,168,128]{2,1,0:T(8,128)(2,1)}), bf16[16,168,128]{2,1,0:T(8,128)(2,1)S(1)}, u32[]{:S(2)}, u32[]{:S(2)}) %all-to-all-start.1) | async-done | bytes 688160 | tf_op jit(solution)/shard_map/all_to_all | solution.py:427
  71.0 1.4 chain.1
  72.4 3.7 %all-to-all-start.2 = ((bf16[16,160,128]{2,1,0:T(8,128)(2,1)}), bf16[16,160,128]{2,1,0:T(8,128)(2,1)S(1)}, u32[]{:S(2)}, u32[]{:S(2)}) async-start(bf16[16,160,128]{2,1,0:T(8,128)(2,1)} %chain.1), calls=%async_computation.2 | async-start | bytes 1310720 | tf_op jit(solution)/shard_map/all_to_all | solution.py:436
  76.9 2.3 %inside_right.1 = (f32[128,1280]{1,0:T(8,128)S(1)}, f32[128,128]{1,0:T(8,128)S(1)}, f32[128,128]{1,0:T(8,128)S(1)}, f32[128,128]{1,0:T(8,128)S(1)}) custom-call(f32[128,128]{1,0:T(8,128)S(1)} %get-tuple-element.24.refs_0_.proj_ref, f32[128,128]{1,0:T(8,128)S(1)} %get-tuple-element.25.refs_1_.pre_ref, f32[128,128]{1,0:T(8,128)S(1)} %get-tuple-element.26.refs_2_.cum_ref, ...), custom_call_target="tpu_custom_call" | custom-call | flops 200000000 | bytes 3000000 | tf_op jit(solution)/shard_map/inside_right/pallas_call | solution.py:388
  81.9 13.6 %all-to-all-done.2.carried_ref = bf16[16,160,128]{2,1,0:T(8,128)(2,1)S(1)} async-done(((bf16[16,160,128]{2,1,0:T(8,128)(2,1)}), bf16[16,160,128]{2,1,0:T(8,128)(2,1)S(1)}, u32[]{:S(2)}, u32[]{:S(2)}) %all-to-all-start.2) | async-done | bytes 655392 | tf_op jit(solution)/shard_map/all_to_all | solution.py:436
  95.5 1.1 copy-done.9
  96.6 0.8 copy-done.13
  99.1 7.2 %last.1 = (bf16[256,256]{1,0:T(8,128)(2,1)S(1)}, bf16[128,2560]{1,0:T(8,128)(2,1)}, f32[32,56,128]{2,1,0:T(8,128)S(1)}, bf16[32,56,128]{2,1,0:T(8,128)(2,1)S(1)}) custom-call(s32[1]{0:T(128)} %bitcast.core_ref, bf16[16,160,128]{2,1,0:T(8,128)(2,1)S(1)} %all-to-all-done.2.carried_ref, f32[128,128]{1,0:T(8,128)S(1)} %get-tuple-element.24.refs_0_.proj_ref, ...), custom_call_target="tpu_custom_call" | custom-call | tf_op jit(solution)/shard_map/last/pallas_call | solution.py:388
  106.9 1.9 %collective-permute-start.1 = (bf16[32,56,128]{2,1,0:T(8,128)(2,1)S(1)}, bf16[32,56,128]{2,1,0:T(8,128)(2,1)S(1)}, u32[]{:S(2)}, u32[]{:S(2)}) collective-permute-start(bf16[32,56,128]{2,1,0:T(8,128)(2,1)S(1)} %get-tuple-element.39), channel_id=1, source_target_pairs={{0,1},{1,0},{2,3},{3,2},{4,5},{5,4},{6,7},{7,6},{8,9},{9,8},{10,11... | collective-permute-start | bytes 1376264 | tf_op jit(solution)/shard_map/ppermute | solution.py:453
  108.8 1.8 %collective-permute-done.1 = bf16[32,56,128]{2,1,0:T(8,128)(2,1)S(1)} collective-permute-done((bf16[32,56,128]{2,1,0:T(8,128)(2,1)S(1)}, bf16[32,56,128]{2,1,0:T(8,128)(2,1)S(1)}, u32[]{:S(2)}, u32[]{:S(2)}) %collective-permute-start.1) | collective-permute-done | bytes 458784 | tf_op jit(solution)/shard_map/ppermute | solution.py:453
  110.6 0.9 add_convert_fusion
  111.5 4.3 %all-to-all-start.3 = ((bf16[32,56,128]{2,1,0:T(8,128)(2,1)}), bf16[32,56,128]{2,1,0:T(8,128)(2,1)S(1)}, u32[]{:S(2)}, u32[]{:S(2)}) async-start(bf16[32,56,128]{2,1,0:T(8,128)(2,1)} %add_convert_fusion), calls=%async_computation.3 | async-start | bytes 917504 | tf_op jit(solution)/shard_map/all_to_all | solution.py:454
  115.9 1.4 back.1
  117.2 13.9 %all-to-all-done.3 = bf16[32,56,128]{2,1,0:T(8,128)(2,1)S(1)} async-done(((bf16[32,56,128]{2,1,0:T(8,128)(2,1)}), bf16[32,56,128]{2,1,0:T(8,128)(2,1)S(1)}, u32[]{:S(2)}, u32[]{:S(2)}) %all-to-all-start.3) | async-done | bytes 458784 | tf_op jit(solution)/shard_map/all_to_all | solution.py:454
  131.3 17.6 %all-gather = f32[896,128]{1,0:T(8,128)S(1)} all-gather(f32[56,128]{1,0:T(8,128)S(1)} %convert_reduce_fusion), channel_id=2, replica_groups=mesh['dp'=32,'seq'=16] {'seq'}, dimensions={0}, use_global_device_ids=true | all-gather | bytes 487424 | tf_op jit(solution)/shard_map/all_gather | solution.py:460
  148.8 1.0 finish.1
  (54 shorter events, 9.2 us)
Async XLA Ops:
  0.6 32.0 %copy-start.1 = (bf16[1,128,2560]{2,1,0:T(8,128)(2,1)S(1)}, bf16[1,128,2560]{2,1,0:T(8,128)(2,1)}, u32[]{:S(2)}) copy-start(bf16[1,128,2560]{2,1,0:T(8,128)(2,1)} %param.10) | copy-start | bytes 1966084
  0.6 32.0 %copy-start = (bf16[1,128,2560]{2,1,0:T(8,128)(2,1)S(1)}, bf16[1,128,2560]{2,1,0:T(8,128)(2,1)}, u32[]{:S(2)}) copy-start(bf16[1,128,2560]{2,1,0:T(8,128)(2,1)} %param.9) | copy-start | bytes 1966084
  2.2 30.4 %copy-start.24 = (f32[40]{0:T(128)S(1)}, f32[40]{0:T(128)}, u32[]{:S(2)}) copy-start(f32[40]{0:T(128)} %param.14) | copy-start | bytes 484
  2.2 30.4 %copy-start.25 = (f32[40]{0:T(128)S(1)}, f32[40]{0:T(128)}, u32[]{:S(2)}) copy-start(f32[40]{0:T(128)} %param.13) | copy-start | bytes 484
  26.6 6.0 %collective-permute-start = (bf16[32,56,128]{2,1,0:T(8,128)(2,1)S(1)}, bf16[32,56,128]{2,1,0:T(8,128)(2,1)S(1)}, u32[]{:S(2)}, u32[]{:S(2)}) collective-permute-start(bf16[32,56,128]{2,1,0:T(8,128)(2,1)S(1)} %all_to_all.20.mine_ref), channel_id=1, source_target_pairs={{0,1},{1,0},{2,3},{3,2},{4,5},{5,4},{6,7},{7,6},{8,9},{9,8},{10,11... | collective-permute-start | bytes 1376264 | tf_op jit(solution)/shard_map/ppermute | solution.py:419
  32.6 1.1 copy-start.2
  38.5 1.1 copy-start.4
  39.6 31.4 %all-to-all-start.1 = ((bf16[16,168,128]{2,1,0:T(8,128)(2,1)}), bf16[16,168,128]{2,1,0:T(8,128)(2,1)S(1)}, u32[]{:S(2)}, u32[]{:S(2)}) async-start(bf16[16,168,128]{2,1,0:T(8,128)(2,1)} %get-tuple-element.23), calls=%async_computation.1 | async-start | bytes 1376256 | tf_op jit(solution)/shard_map/all_to_all | solution.py:427
  52.6 0.8 copy-start.6
  54.0 18.4 %copy-start.20 = (f32[128,128]{1,0:T(8,128)}, f32[128,128]{1,0:T(8,128)S(1)}, u32[]{:S(2)}) copy-start(f32[128,128]{1,0:T(8,128)S(1)} %get-tuple-element.30.refs_7_) | copy-start | bytes 196612
  54.0 22.0 %copy-start.3 = (bf16[1,128,2560]{2,1,0:T(8,128)(2,1)S(1)}, bf16[1,128,2560]{2,1,0:T(8,128)(2,1)}, u32[]{:S(2)}) copy-start(bf16[1,128,2560]{2,1,0:T(8,128)(2,1)} %param.8) | copy-start | bytes 1966084
  72.4 23.1 %all-to-all-start.2 = ((bf16[16,160,128]{2,1,0:T(8,128)(2,1)}), bf16[16,160,128]{2,1,0:T(8,128)(2,1)S(1)}, u32[]{:S(2)}, u32[]{:S(2)}) async-start(bf16[16,160,128]{2,1,0:T(8,128)(2,1)} %chain.1), calls=%async_computation.2 | async-start | bytes 1310720 | tf_op jit(solution)/shard_map/all_to_all | solution.py:436
  76.1 0.8 copy-start.19
  76.1 0.9 copy-start.21
  76.1 19.4 %copy-start.26 = (f32[40]{0:T(128)S(1)}, f32[40]{0:T(128)}, u32[]{:S(2)}) copy-start(f32[40]{0:T(128)} %param.15) | copy-start | bytes 484
  76.3 19.1 %copy-start.7 = (f32[128,1280]{1,0:T(8,128)S(1)}, f32[128,1280]{1,0:T(8,128)}, u32[]{:S(2)}) copy-start(f32[128,1280]{1,0:T(8,128)} %copy-done.6) | copy-start | bytes 1966084
  95.5 1.1 copy-start.9
  96.6 0.8 copy-start.13
  97.4 0.8 copy-start.15
  98.2 0.8 copy-start.17
  106.9 3.7 %collective-permute-start.1 = (bf16[32,56,128]{2,1,0:T(8,128)(2,1)S(1)}, bf16[32,56,128]{2,1,0:T(8,128)(2,1)S(1)}, u32[]{:S(2)}, u32[]{:S(2)}) collective-permute-start(bf16[32,56,128]{2,1,0:T(8,128)(2,1)S(1)} %get-tuple-element.39), channel_id=1, source_target_pairs={{0,1},{1,0},{2,3},{3,2},{4,5},{5,4},{6,7},{7,6},{8,9},{9,8},{10,11... | collective-permute-start | bytes 1376264 | tf_op jit(solution)/shard_map/ppermute | solution.py:453
  110.6 5.2 %copy-start.5 = (bf16[2560,256]{1,0:T(8,128)(2,1)S(1)}, bf16[2560,256]{1,0:T(8,128)(2,1)}, u32[]{:S(2)}) copy-start(bf16[2560,256]{1,0:T(8,128)(2,1)} %copy-done.4) | copy-start | bytes 3932164
  110.6 5.2 %copy-start.11 = (bf16[256,256]{1,0:T(8,128)(2,1)S(1)}, bf16[256,256]{1,0:T(8,128)(2,1)}, u32[]{:S(2)}) copy-start(bf16[256,256]{1,0:T(8,128)(2,1)} %copy-done.10) | copy-start | bytes 393220
  111.5 19.6 %all-to-all-start.3 = ((bf16[32,56,128]{2,1,0:T(8,128)(2,1)}), bf16[32,56,128]{2,1,0:T(8,128)(2,1)S(1)}, u32[]{:S(2)}, u32[]{:S(2)}) async-start(bf16[32,56,128]{2,1,0:T(8,128)(2,1)} %add_convert_fusion), calls=%async_computation.3 | async-start | bytes 917504 | tf_op jit(solution)/shard_map/all_to_all | solution.py:454
  (8 other events, 5.5 us)

commit v3 on v2

--- a/solution.py
+++ b/solution.py
@@ -1,5 +1,4 @@
 import math
-from functools import partial
 
 import jax
 import jax.numpy as jnp
@@ -73,13 +72,13 @@
     return jnp.where(lane < 40, first, jnp.where(lane < 80, second, third)).astype(bf16)
 
 
-def spread_matrix(pair):
-    k, lane = iota((LANES, LANES), 0), iota((LANES, LANES), 1)
+def spread_matrix(pair, pairs=1):
+    k, lane = iota((LANES, LANES * pairs), 0), iota((LANES, LANES * pairs), 1)
     return ones_where(head_of_lane(k) == 2 * pair + (lane >> 6), bf16)
 
 
-def gather_matrix(pair):
-    lane, k = iota((LANES, LANES), 0), iota((LANES, LANES), 1)
+def gather_matrix(pair, pairs=1):
+    lane, k = iota((LANES * pairs, LANES), 0), iota((LANES * pairs, LANES), 1)
     return ones_where(head_of_lane(k) == 2 * pair + (lane >> 6), bf16)
 
 
@@ -102,9 +101,11 @@
 
 
 def first_kernel(
-    core_ref, mine_ref, other_ref, feat_ref, x_ref, g_ref, bias_ref, rate_ref,
-    weight_ref, proj_ref, pre_ref, cum_ref, state_ref,
+    core_ref, mine_ref, other_ref, feat_hbm, x_ref, g_ref, bias_ref, rate_ref,
+    weight_hbm, small_ref, state_ref, weight_ref, feat_ref, sems,
 ):
+    fetch = pltpu.make_async_copy(feat_hbm, feat_ref, sems.at[0])
+    fetch.start()
     lane16 = iota((16, LANES), 1)
     group = [
         ones_where((lane16 >= 40 * k) & (lane16 < 40 * k + 40), bf16) for k in range(3)
@@ -132,6 +133,9 @@
     def _():
         assemble(other_ref, mine_ref)
 
+    store = pltpu.make_async_copy(weight_ref, weight_hbm, sems.at[1])
+    store.start()
+    fetch.wait()
     both = lax.dot_general(feat_ref[...], weight_ref[...], NN, preferred_element_type=f32)
     proj = both[:, 0:LANES]
     row, lane = iota((LANES, LANES), 0), iota((LANES, LANES), 1)
@@ -140,36 +144,42 @@
     pre = mm_exact(both[:, LANES:], fold) + triple(bias_ref[...])
     step = jnp.maximum(pre, 0.0) + jnp.log1p(jnp.exp(-jnp.abs(pre)))
     cum = mm_exact(ones_where(row >= lane), -triple(rate_ref[...]) * step)
-    proj_ref[...] = proj
-    pre_ref[...] = pre
-    cum_ref[...] = cum
+    small_ref[0] = proj
+    small_ref[1] = pre
+    small_ref[2] = cum
     total = cum[TOK - 1 : TOK]
     stacked = jnp.concatenate(
         [split(step * jnp.exp(total - cum)), split(jnp.exp(cum))], axis=0
     )
     turned_high, turned_low = high_low(proj.T)
     both_turned = jnp.concatenate([turned_high, turned_low], axis=0)
-    forward = (row & 7) < 4
-
-    def block(pair):
-        cols = slice(LANES * pair, LANES * pair + LANES)
-        wide = lax.dot_general(stacked, spread_matrix(pair), NN, preferred_element_type=f32)
-        ending = x_ref[:, cols].astype(f32) * wide[0:TOK]
-        weighted = g_ref[:, cols].astype(f32) * wide[TOK:]
-        high, low = high_low(jnp.concatenate([ending, weighted], axis=1))
-        joined = mm(both_turned, high)
-        joined = joined[0:LANES] + (joined[LANES:] + mm(turned_high, low))
-        return jnp.where(forward, joined[:, 0:LANES], joined[:, LANES:]).reshape(SEQ, 8, LANES)
+    forward = (iota((LANES, 2 * LANES), 0) & 7) < 4
 
     for two in range(PAIRS // 2):
-        value = jnp.concatenate([block(2 * two), block(2 * two + 1)], axis=1)
+        cols = slice(256 * two, 256 * two + 256)
+        wide = lax.dot_general(
+            stacked, spread_matrix(2 * two, 2), NN, preferred_element_type=f32
+        )
+        ending = high_low(x_ref[:, cols].astype(f32) * wide[0:TOK])
+        weighted = high_low(g_ref[:, cols].astype(f32) * wide[TOK:])
+
+        def product(halves):
+            value = mm(both_turned, halves[0])
+            return value[0:LANES] + (value[LANES:] + mm(turned_high, halves[1]))
+
+        chosen = jnp.where(forward, product(ending), product(weighted))
+        value = jnp.concatenate(
+            [chosen[:, k * LANES : k * LANES + LANES].reshape(SEQ, 8, LANES) for k in range(2)],
+            axis=1,
+        )
         state_ref[:, 16 * two : 16 * two + 16, :] = value.astype(bf16)
     decay = split(jnp.broadcast_to(total, (8, LANES)))
     for owner in range(SEQ):
         state_ref[owner, 160:168, :] = decay
-
-
-def chain_kernel(state_ref, after_ref, out_ref):
+    store.wait()
+
+
+def chain_kernel(state_ref, out_ref):
     row16 = iota((16, LANES), 0)
     logs = jnp.zeros((16, LANES), f32)
     for place in range(SEQ):
@@ -209,11 +219,9 @@
     return jnp.maximum(pre, 0.0) + jnp.log1p(jnp.exp(-jnp.abs(pre)))
 
 
-def inside_kernel(first_pair, start, *refs):
-    proj_ref, pre_ref, cum_ref, x_ref, g_ref = refs[:5]
-    scaled_ref, across_ref, own_ref, rows_ref = refs[-4:]
-    proj, cum = proj_ref[...], cum_ref[...]
-    step = softplus(pre_ref[...])
+def inside_kernel(small_ref, x_ref, g_ref, scaled_hbm, sums_ref, scaled_ref, sem):
+    proj, cum = small_ref[0], small_ref[2]
+    step = softplus(small_ref[1])
     row, lane = iota((LANES, LANES), 0), iota((LANES, LANES), 1)
     low = (lane & 7) < 4
     b_low = jnp.where(low, proj, 0.0)
@@ -222,16 +230,12 @@
     causal = lane >= row
     cum_turned = cum.T
     lane_head = head_of_lane(lane)
-    if start:
-        across = jnp.zeros((TOK, TOK), f32)
-        own = jnp.zeros((TOK, LANES), f32)
-        rows_ref[...] = jnp.zeros_like(rows_ref)
-    else:
-        across, own = refs[5][...], refs[6][...]
-        rows_ref[...] = refs[7][...]
+    across = jnp.zeros((TOK, TOK), f32)
+    own = jnp.zeros((TOK, LANES), f32)
+    sums_ref[2] = jnp.zeros((LANES, TOK), f32)
     first_half = ones_where(lane < 64, bf16)
     second_half = ones_where(lane >= 64, bf16)
-    for pair in range(first_pair, first_pair + PAIRS // 2):
+    for pair in range(PAIRS):
         cols = slice(LANES * pair, LANES * pair + LANES)
         x, g = x_ref[:, cols], g_ref[:, cols]
         mixed, parts = [], []
@@ -246,24 +250,29 @@
             across = across + spot * step_col
             product = spot * meet
             own = jnp.where(lane_head == head, jnp.sum(product, axis=1, keepdims=True), own)
-            rows_ref[head : head + 1, :] = jnp.sum(product * step_col, axis=0, keepdims=True)
+            sums_ref[2, head : head + 1, :] = jnp.sum(product * step_col, axis=0, keepdims=True)
             mixed.append((meet * weight).astype(bf16))
             parts.append(g_half)
-        here = slice(LANES * (pair - first_pair), LANES * (pair - first_pair) + LANES)
-        scaled_ref[:, here] = lax.dot_general(
+        scaled_ref[:, cols] = lax.dot_general(
             jnp.concatenate(mixed, axis=1), jnp.concatenate(parts, axis=0), NN,
             preferred_element_type=f32,
         )
-    across_ref[...] = across
-    own_ref[...] = own
+    sums_ref[0] = across
+    sums_ref[1] = own
+    store = pltpu.make_async_copy(scaled_ref, scaled_hbm, sem)
+    store.start()
+    store.wait()
 
 
 def last_kernel(
-    core_ref, carried_ref, proj_ref, pre_ref, cum_ref, left_ref, right_ref, across_ref,
-    own_ref, rows_ref, turned_ref, x_ref, g_ref, rate_ref, skip_ref,
+    core_ref, carried_ref, small_ref, scaled_hbm, inner_ref, turned_ref, x_ref, g_ref,
+    rate_ref, skip_ref,
     grads_ref, head_grad_ref, keep_ref, send_ref,
+    scaled_ref, state_all, lines_all, terms_all, select_all, sem,
 ):
-    proj, pre, cum = proj_ref[...], pre_ref[...], cum_ref[...]
+    fetch = pltpu.make_async_copy(scaled_hbm, scaled_ref, sem)
+    fetch.start()
+    proj, pre, cum = small_ref[0], small_ref[1], small_ref[2]
     step = softplus(pre)
     total = cum[TOK - 1 : TOK]
     row, lane = iota((LANES, LANES), 0), iota((LANES, LANES), 1)
@@ -281,43 +290,56 @@
         ],
         axis=0,
     )
-    crossed = jnp.zeros((4 * TOK, LANES), f32)
-    sums = jnp.zeros((4 * TOK + 32, LANES), f32)
-    low_rows = (row & 7) < 4
+    low_rows = (iota((LANES, 2 * LANES), 0) & 7) < 4
     for two in range(PAIRS // 2):
+        cols = slice(256 * two, 256 * two + 256)
+        later_cols = slice(WIDE + 256 * two, WIDE + 256 * two + 256)
         chunk = carried_ref[:, 16 * two : 16 * two + 16, :].astype(f32)
-        for which in range(2):
-            pair = 2 * two + which
-            cols = slice(LANES * pair, LANES * pair + LANES)
-            state = chunk[:, 8 * which : 8 * which + 8, :].reshape(LANES, LANES)
-            state_b = state.astype(bf16)
-            wide = lax.dot_general(stacked, spread_matrix(pair), NN, preferred_element_type=f32)
-            step_w, end_w, start_w = wide[0:TOK], wide[TOK : 2 * TOK], wide[2 * TOK : 3 * TOK]
-            skip_w = wide[3 * TOK : 3 * TOK + 1]
-            x, g = x_ref[:, cols].astype(f32), g_ref[:, cols].astype(f32)
-            weighted = g * start_w
-            ending = x * end_w
-            pushed = lax.dot_general(left, state_b, NN, preferred_element_type=f32)
-            pushed = pushed[0 : 2 * TOK] + pushed[2 * TOK :]
-            out, reach = pushed[0:TOK], pushed[TOK:]
-            lines = jnp.concatenate([weighted, ending * step_w], axis=0)
-            crossed = crossed + mm(jnp.concatenate(high_low(lines), axis=0), state_b, NT)
-            pairing = jnp.where(low_rows, state * pltpu.roll(state, LANES - 4, 0), 0.0)
-            pairing = jnp.sum(pairing.reshape(SEQ, 8, LANES), axis=0)
-            pairing = jnp.concatenate([pairing, jnp.zeros((8, LANES), f32)], axis=0)
-            lines = jnp.concatenate([weighted * out, ending * reach, pairing], axis=0)
-            sums = sums + mm(jnp.concatenate(high_low(lines), axis=0), gather_matrix(pair))
-            half_ref = left_ref if two < 5 else right_ref
-            first_lane = LANES * (pair % 10)
-            whole = half_ref[:, first_lane : first_lane + LANES] + end_w * reach
-            head_grad_ref[:, cols] = (g * skip_w + step_w * whole).astype(bf16)
-    crossed = crossed[0 : 2 * TOK] + crossed[2 * TOK :]
-    sums = sums[0 : 2 * TOK + 16] + sums[2 * TOK + 16 :]
+        state = jnp.concatenate(
+            [chunk[:, 8 * k : 8 * k + 8, :].reshape(LANES, LANES) for k in range(2)], axis=1
+        )
+        state_b = state.astype(bf16)
+        state_all[:, cols] = state_b
+        select_all[cols, :] = gather_matrix(2 * two, 2)
+        wide = lax.dot_general(
+            stacked, spread_matrix(2 * two, 2), NN, preferred_element_type=f32
+        )
+        step_w, end_w, start_w = wide[0:TOK], wide[TOK : 2 * TOK], wide[2 * TOK : 3 * TOK]
+        skip_w = wide[3 * TOK : 3 * TOK + 1]
+        x, g = x_ref[:, cols].astype(f32), g_ref[:, cols].astype(f32)
+        weighted = g * start_w
+        ending = x * end_w
+        pushed = lax.dot_general(left, state_b, NN, preferred_element_type=f32)
+        pushed = pushed[0 : 2 * TOK] + pushed[2 * TOK :]
+        out, reach = pushed[0:TOK], pushed[TOK:]
+        high, low_part = high_low(jnp.concatenate([weighted, ending * step_w], axis=0))
+        lines_all[:, cols] = high
+        lines_all[:, later_cols] = low_part
+        pairing = jnp.where(low_rows, state * pltpu.roll(state, LANES - 4, 0), 0.0)
+        pairing = jnp.sum(pairing.reshape(SEQ, 8, 2 * LANES), axis=0)
+        pairing = jnp.concatenate([pairing, jnp.zeros((8, 2 * LANES), f32)], axis=0)
+        high, low_part = high_low(
+            jnp.concatenate([weighted * out, ending * reach, pairing], axis=0)
+        )
+        terms_all[:, cols] = high
+        terms_all[:, later_cols] = low_part
+        if two == 0:
+            fetch.wait()
+        whole = scaled_ref[:, cols] + end_w * reach
+        head_grad_ref[:, cols] = (g * skip_w + step_w * whole).astype(bf16)
+
+    def both_parts(ref, right, dims):
+        return lax.dot_general(
+            ref[:, 0:WIDE], right, dims, preferred_element_type=f32
+        ) + lax.dot_general(ref[:, WIDE:], right, dims, preferred_element_type=f32)
+
+    crossed = both_parts(lines_all, state_all[...], NT)
+    sums = both_parts(terms_all, select_all[...], NN)
     through, reached = sums[0:TOK], sums[TOK : 2 * TOK]
     paired = jnp.sum(sums[2 * TOK : 2 * TOK + 8], axis=0, keepdims=True)
-    own = own_ref[...]
+    own = inner_ref[1]
     lane_head = head_of_lane(lane)
-    later = mm_exact(rows_ref[...].T, ones_where((row == lane_head) & (row < HEADS)))
+    later = mm_exact(inner_ref[2].T, ones_where((row == lane_head) & (row < HEADS)))
     decay_grad = (
         mm_exact(ones_where(lane >= row), later - step * own + through)
         + mm_exact(ones_where(lane < row), step * reached)
@@ -326,7 +348,7 @@
     step_grad = own + reached - triple(rate_ref[...]) * decay_grad
     pre_grad = step_grad * jax.nn.sigmoid(pre)
     pre_grad = jnp.where(lane < 3 * HEADS, pre_grad, 0.0)
-    across = across_ref[...]
+    across = inner_ref[0]
     bc_grad = mm_exact(across, c_low) + mm_exact(across.T, b_high)
     bc_grad = bc_grad + jnp.where(
         low, pltpu.roll(crossed[TOK:], LANES - 4, 1), pltpu.roll(crossed[0:TOK], 4, 1)
@@ -356,12 +378,18 @@
             send_ref[owner] = jnp.where(first_core, two, one).astype(bf16)
 
 
-def back_kernel(grads_ref, weight_ref, input_grad_ref):
+def back_kernel(grads_ref, weight_ref, input_grad_ref, token_ref):
+    token_ref[...] = jnp.zeros_like(token_ref)
     tall = grads_ref[...]
     for part in range(10):
         cols = slice(256 * part, 256 * part + 256)
         product = lax.dot_general(tall, weight_ref[cols, :], NT, preferred_element_type=f32)
         input_grad_ref[:, cols] = (product[0:TOK] + product[TOK:]).astype(bf16)
+
+
+def join_kernel(keep_ref, other_ref, token_ref, out_ref):
+    for owner in range(DP):
+        out_ref[owner] = (keep_ref[owner] + other_ref[owner].astype(f32)).astype(bf16)
 
 
 def finish_kernel(parts_ref, bc_ref, dt_ref):
@@ -382,20 +410,32 @@
         )
 
 
-def call(kernel, name, out_shape, scalars, arrays, scratch=(), flops=0, bytes_accessed=0):
+def call(kernel, name, out_shape, scalars, arrays, in_hbm=(), out_hbm=(), **options):
     smem = pl.BlockSpec(memory_space=pltpu.SMEM)
     vmem = pl.BlockSpec(memory_space=pltpu.VMEM)
+    hbm = pl.BlockSpec(memory_space=pltpu.HBM)
+    flops, moved = options.pop("cost", (0, 0))
+    several = isinstance(out_shape, tuple)
+    if out_hbm:
+        out_shape = tuple(
+            pltpu.HBM(part.shape, part.dtype) if k in out_hbm else part
+            for k, part in enumerate(out_shape)
+        )
+    arrays = [
+        pltpu.with_memory_space_constraint(part, pltpu.HBM) if k in in_hbm else part
+        for k, part in enumerate(arrays)
+    ]
+    out_specs = [hbm if k in out_hbm else vmem for k in range(len(out_shape))] if several else vmem
     return pl.pallas_call(
         kernel,
         name=name,
         out_shape=out_shape,
-        in_specs=[smem] * len(scalars) + [vmem] * len(arrays),
-        out_specs=jax.tree.map(lambda _: vmem, out_shape),
-        scratch_shapes=scratch,
-        compiler_params=pltpu.CompilerParams(vmem_limit_bytes=20 << 20),
-        cost_estimate=pl.CostEstimate(
-            flops=flops, bytes_accessed=bytes_accessed, transcendentals=0
-        ),
+        in_specs=[smem] * len(scalars)
+        + [hbm if k in in_hbm else vmem for k in range(len(arrays))],
+        out_specs=tuple(out_specs) if several else out_specs,
+        scratch_shapes=options.pop("scratch", ()),
+        compiler_params=pltpu.CompilerParams(vmem_limit_bytes=40 << 20),
+        cost_estimate=pl.CostEstimate(flops=flops, bytes_accessed=moved, transcendentals=0),
     )(*scalars, *arrays)
 
 
@@ -410,34 +450,41 @@
     core = (lax.axis_index("seq") & 1).astype(jnp.int32).reshape(1)
     feats, x, g = features[0], head_inputs[0], out_grad[0]
     bias, rate, skip = dt_bias[None], decay_rate[None], skip_gain[None]
-    square = shape((TOK, LANES), f32)
     chunks = shape((DP, HALF, LANES), bf16)
+    three = shape((3, TOK, LANES), f32)
+    dma = pltpu.SemaphoreType.DMA
 
     sent = call(pack_kernel, "pack", chunks, [core], [bc_weight, dt_weight.T])
     mine = lax.all_to_all(sent, "dp", 0, 0, tiled=True)
-    turned = call(turn_kernel, "turn", shape((WIDE, TOK), bf16), [], [feats], bytes_accessed=2_000_000)
     other = lax.ppermute(mine, "seq", SWAP)
-    weight, proj, pre, cum, local = call(
+    weight, small, local = call(
         first_kernel,
         "first",
-        (shape((WIDE, 2 * LANES), bf16), square, square, square, shape((SEQ, 168, LANES), bf16)),
+        (shape((WIDE, 2 * LANES), bf16), three, shape((SEQ, 168, LANES), bf16)),
         [core],
         [mine, other, feats, x, g, bias, rate],
+        in_hbm=(2,),
+        out_hbm=(0,),
+        scratch=[
+            pltpu.VMEM((WIDE, 2 * LANES), bf16),
+            pltpu.VMEM((TOK, WIDE), bf16),
+            dma((2,)),
+        ],
     )
     gathered = lax.all_to_all(local, "seq", 0, 0, tiled=True)
-    half = (shape((TOK, WIDE // 2), f32), square, square, square)
-    cost = dict(flops=200_000_000, bytes_accessed=3_000_000)
-    left, across, own, rows = call(
-        partial(inside_kernel, 0, True), "inside_left", half, [], [proj, pre, cum, x, g], **cost
-    )
-    entering = call(
-        chain_kernel, "chain", shape((SEQ, 160, LANES), bf16), [], [gathered, across[0:8]]
-    )
+    entering = call(chain_kernel, "chain", shape((SEQ, 160, LANES), bf16), [], [gathered])
     carried = lax.all_to_all(entering, "seq", 0, 0, tiled=True)
-    right, across, own, rows = call(
-        partial(inside_kernel, PAIRS // 2, False), "inside_right", half, [],
-        [proj, pre, cum, x, g, across, own, rows], **cost,
-    )
+    scaled, inner = call(
+        inside_kernel,
+        "inside",
+        (shape((TOK, WIDE), f32), three),
+        [],
+        [small, x, g],
+        out_hbm=(0,),
+        scratch=[pltpu.VMEM((TOK, WIDE), f32), dma],
+        cost=(400_000_000, 4_000_000),
+    )
+    turned = call(turn_kernel, "turn", shape((WIDE, TOK), bf16), [], [feats], cost=(0, 2_000_000))
     grads, head_grad, keep, send = call(
         last_kernel,
         "last",
@@ -448,14 +495,28 @@
             chunks,
         ),
         [core],
-        [carried, proj, pre, cum, left, right, across, own, rows, turned, x, g, rate, skip],
-    )
-    paired = (keep + lax.ppermute(send, "seq", SWAP).astype(f32)).astype(bf16)
+        [carried, small, scaled, inner, turned, x, g, rate, skip],
+        in_hbm=(2,),
+        scratch=[
+            pltpu.VMEM((TOK, WIDE), f32),
+            pltpu.VMEM((LANES, WIDE), bf16),
+            pltpu.VMEM((2 * TOK, 2 * WIDE), bf16),
+            pltpu.VMEM((2 * TOK + 16, 2 * WIDE), bf16),
+            pltpu.VMEM((WIDE, LANES), bf16),
+            dma,
+        ],
+    )
+    other = lax.ppermute(send, "seq", SWAP)
+    input_grad, token = call(
+        back_kernel,
+        "back",
+        (shape((TOK, WIDE), bf16), shape((8, LANES), f32)),
+        [],
+        [grads, weight],
+        cost=(340_000_000, 3_000_000),
+    )
+    paired = call(join_kernel, "join", chunks, [], [keep, other, token])
     owned = lax.all_to_all(paired, "dp", 0, 0, tiled=True)
-    input_grad = call(
-        back_kernel, "back", shape((TOK, WIDE), bf16), [], [grads, weight],
-        flops=340_000_000, bytes_accessed=3_000_000,
-    )
     owned = jnp.sum(owned.astype(f32), axis=0)
     parts = lax.all_gather(owned, "seq")
     bc_grad, dt_grad = call(

time: 151 us -> 142 us (0.940)
  blocking collectives: 41.7 us -> 93.4 us
  waiting for transfers between devices: 47.6 us -> 13.9 us
  starting transfers between devices: 25.2 us -> 10.3 us
  local copies, waits for them, and re-layouts: 12.7 us -> 1.55 us
    all_to_all x0 -> x2, blocking collectives: none -> 50.8 us  [the longest x1 31.4 us: body(): gathered = lax.all_to_all(local, 'seq', 0, 0, tiled=True)]
    all_to_all x2 -> x0, waiting for transfers between devices: 30.9 us -> none  [the longest x1 16.9 us: body(): gathered = lax.all_to_all(local, 'seq', 0, 0, tiled=True)]
    all_to_all x2 -> x0, starting transfers between devices: 15 us -> none  [the longest x1 10.7 us: body(): gathered = lax.all_to_all(local, 'seq', 0, 0, tiled=True)]
    unnamed x54 -> x18, local copies, waits for them, and re-layouts: 12.7 us -> 1.55 us
  transfers between devices with their start and end apart: 5 -> 3, of which waited for: 5 -> 3; matrix products, arithmetic and copies ran while one was open for 0% -> 0% of each run, Pallas kernels for 4% -> 5%
where the time goes in v3:
time: 142 us; the launch traced here: 141 us
  blocking collectives  93.4 us (66%)
  Pallas kernels  21.4 us (15%)
  waiting for transfers between devices  13.9 us (10%)
  starting transfers between devices  10.3 us (7%)
  local copies, waits for them, and re-layouts  1.55 us (1%)
    all_to_all x1, blocking collectives, body(): gathered = lax.all_to_all(local, 'seq', 0, 0, tiled=True)  31.4 us
    all_to_all x1, blocking collectives, body(): mine = lax.all_to_all(sent, 'dp', 0, 0, tiled=True)  24.1 us
    pallas_call x9, Pallas kernels, call(): pl.pallas_call(kernel, name=name, out_shape=out_shape, in_specs=[smem] *...  21.4 us
    all_to_all x1, blocking collectives, body(): owned = lax.all_to_all(paired, 'dp', 0, 0, tiled=True)  19.4 us
    all_gather x1, blocking collectives, body(): parts = lax.all_gather(owned, 'seq')  18.4 us
    all_to_all x1, waiting for transfers between devices, body(): carried = lax.all_to_all(entering, 'seq', 0, 0, tiled=True)  12.2 us
    ppermute x1, starting transfers between devices, body(): other = lax.ppermute(mine, 'seq', SWAP)  4.59 us
    all_to_all x1, starting transfers between devices, body(): carried = lax.all_to_all(entering, 'seq', 0, 0, tiled=True)  3.67 us
  transfers between devices with their start and end apart: 3, of which 3 were waited for; matrix products, arithmetic and copies ran while one was open for 0% of the time, Pallas kernels for 5%

profile of v3, /device:TPU:9, one launch (start us, length us, event | category | flops | bytes accessed | tf_op | source)
XLA Modules:
  0.0 141.3 jit_solution(10477065833727096280)
XLA Ops:
  0.7 0.8 copy-done.4
  1.5 0.7 copy-done.5
  2.2 0.2 pack.1
  2.4 24.1 %all_to_all.20.mine_ref = bf16[32,56,128]{2,1,0:T(8,128)(2,1)S(1)} all-to-all(bf16[32,56,128]{2,1,0:T(8,128)(2,1)S(1)} %pack.1), channel_id=1, replica_groups=mesh['dp'=32,'seq'=16] {'dp'}, dimensions={0} | all-to-all | bytes 917504 | tf_op jit(solution)/shard_map/all_to_all | solution.py:458
  26.6 4.6 %collective-permute-start = (bf16[32,56,128]{2,1,0:T(8,128)(2,1)S(1)}, bf16[32,56,128]{2,1,0:T(8,128)(2,1)S(1)}, u32[]{:S(2)}, u32[]{:S(2)}) collective-permute-start(bf16[32,56,128]{2,1,0:T(8,128)(2,1)S(1)} %all_to_all.20.mine_ref), channel_id=1, source_target_pairs={{0,1},{1,0},{2,3},{3,2},{4,5},{5,4},{6,7},{7,6},{8,9},{9,8},{10,11... | collective-permute-start | bytes 1376264 | tf_op jit(solution)/shard_map/ppermute | solution.py:459
  31.2 1.4 %collective-permute-done.other_ref = bf16[32,56,128]{2,1,0:T(8,128)(2,1)S(1)} collective-permute-done((bf16[32,56,128]{2,1,0:T(8,128)(2,1)S(1)}, bf16[32,56,128]{2,1,0:T(8,128)(2,1)S(1)}, u32[]{:S(2)}, u32[]{:S(2)}) %collective-permute-start) | collective-permute-done | bytes 458784 | tf_op jit(solution)/shard_map/ppermute | solution.py:459
  32.6 0.0 copy-done.6
  32.6 4.9 %first.1 = (bf16[2560,256]{1,0:T(8,128)(2,1)}, f32[3,128,128]{2,1,0:T(8,128)S(1)}, bf16[16,168,128]{2,1,0:T(8,128)(2,1)S(1)}) custom-call(s32[1]{0:T(128)} %bitcast.core_ref, bf16[32,56,128]{2,1,0:T(8,128)(2,1)S(1)} %all_to_all.20.mine_ref, bf16[32,56,128]{2,1,0:T(8,128)(2,1)S(1)} %collective-permute-done.other_ref, bf16[128,2560]{1,0:T(8,128)(2,1)} %bitcast.18, ...), custom_call_target="tpu_custom_call" | custom-call | tf_op jit(solution)/shard_map/first/pallas_call | solution.py:429
  37.6 31.4 %all_to_all.21.state_ref = bf16[16,168,128]{2,1,0:T(8,128)(2,1)S(1)} all-to-all(bf16[16,168,128]{2,1,0:T(8,128)(2,1)S(1)} %get-tuple-element.17), channel_id=1, replica_groups=mesh['dp'=32,'seq'=16] {'seq'}, dimensions={0} | all-to-all | bytes 1376256 | tf_op jit(solution)/shard_map/all_to_all | solution.py:474
  68.9 1.4 %chain.1 = bf16[16,160,128]{2,1,0:T(8,128)(2,1)} custom-call(bf16[16,168,128]{2,1,0:T(8,128)(2,1)S(1)} %all_to_all.21.state_ref), custom_call_target="tpu_custom_call" | custom-call | tf_op jit(solution)/shard_map/chain/pallas_call | solution.py:429
  70.3 3.7 %all-to-all-start.2 = ((bf16[16,160,128]{2,1,0:T(8,128)(2,1)}), bf16[16,160,128]{2,1,0:T(8,128)(2,1)S(1)}, u32[]{:S(2)}, u32[]{:S(2)}) async-start(bf16[16,160,128]{2,1,0:T(8,128)(2,1)} %chain.1), calls=%async_computation.2 | async-start | bytes 1310720 | tf_op jit(solution)/shard_map/all_to_all | solution.py:476
  74.0 0.0 copy-start.8
  74.0 0.2 turn.1.turned_ref
  74.3 5.6 %inside.1 = (f32[128,2560]{1,0:T(8,128)}, f32[3,128,128]{2,1,0:T(8,128)S(1)}) custom-call(f32[3,128,128]{2,1,0:T(8,128)S(1)} %get-tuple-element.18.small_ref, bf16[128,2560]{1,0:T(8,128)(2,1)S(1)} %bitcast.13, bf16[128,2560]{1,0:T(8,128)(2,1)S(1)} %bitcast.16), custom_call_target="tpu_custom_call" | custom-call | flops 400000000 | bytes 4000000 | tf_op jit(solution)/shard_map/inside/pallas_call | solution.py:429
  79.9 12.2 %all-to-all-done.2.carried_ref = bf16[16,160,128]{2,1,0:T(8,128)(2,1)S(1)} async-done(((bf16[16,160,128]{2,1,0:T(8,128)(2,1)}), bf16[16,160,128]{2,1,0:T(8,128)(2,1)S(1)}, u32[]{:S(2)}, u32[]{:S(2)}) %all-to-all-start.2) | async-done | bytes 655392 | tf_op jit(solution)/shard_map/all_to_all | solution.py:476
  92.1 6.5 %last.1 = (bf16[256,256]{1,0:T(8,128)(2,1)S(1)}, bf16[128,2560]{1,0:T(8,128)(2,1)}, f32[32,56,128]{2,1,0:T(8,128)S(1)}, bf16[32,56,128]{2,1,0:T(8,128)(2,1)S(1)}) custom-call(s32[1]{0:T(128)} %bitcast.core_ref, bf16[16,160,128]{2,1,0:T(8,128)(2,1)S(1)} %all-to-all-done.2.carried_ref, f32[3,128,128]{2,1,0:T(8,128)S(1)} %get-tuple-element.18.small_ref, ...), custom_call_target="tpu_custom_call" | custom-call | tf_op jit(solution)/shard_map/last/pallas_call | solution.py:429
  98.6 2.0 %collective-permute-start.1 = (bf16[32,56,128]{2,1,0:T(8,128)(2,1)S(1)}, bf16[32,56,128]{2,1,0:T(8,128)(2,1)S(1)}, u32[]{:S(2)}, u32[]{:S(2)}) collective-permute-start(bf16[32,56,128]{2,1,0:T(8,128)(2,1)S(1)} %get-tuple-element.26), channel_id=1, source_target_pairs={{0,1},{1,0},{2,3},{3,2},{4,5},{5,4},{6,7},{7,6},{8,9},{9,8},{10,11... | collective-permute-start | bytes 1376264 | tf_op jit(solution)/shard_map/ppermute | solution.py:509
  100.6 1.4 back.1
  102.0 0.3 collective-permute-done.1.other_ref
  102.3 0.1 join.1
  102.4 19.4 %all_to_all.22 = bf16[32,56,128]{2,1,0:T(8,128)(2,1)S(1)} all-to-all(bf16[32,56,128]{2,1,0:T(8,128)(2,1)S(1)} %join.1), channel_id=1, replica_groups=mesh['dp'=32,'seq'=16] {'dp'}, dimensions={0} | all-to-all | bytes 917504 | tf_op jit(solution)/shard_map/all_to_all | solution.py:519
  121.8 0.1 convert_reduce_fusion
  121.9 18.4 %all-gather = f32[896,128]{1,0:T(8,128)S(1)} all-gather(f32[56,128]{1,0:T(8,128)S(1)} %convert_reduce_fusion), channel_id=2, replica_groups=mesh['dp'=32,'seq'=16] {'seq'}, dimensions={0}, use_global_device_ids=true | all-gather | bytes 487424 | tf_op jit(solution)/shard_map/all_gather | solution.py:521
  140.3 1.0 finish.1
  (14 shorter events, 0.0 us)
Async XLA Ops:
  0.6 32.0 %copy-start.1 = (bf16[1,128,2560]{2,1,0:T(8,128)(2,1)S(1)}, bf16[1,128,2560]{2,1,0:T(8,128)(2,1)}, u32[]{:S(2)}) copy-start(bf16[1,128,2560]{2,1,0:T(8,128)(2,1)} %param.10) | copy-start | bytes 1966084
  0.6 32.0 %copy-start = (bf16[1,128,2560]{2,1,0:T(8,128)(2,1)S(1)}, bf16[1,128,2560]{2,1,0:T(8,128)(2,1)}, u32[]{:S(2)}) copy-start(bf16[1,128,2560]{2,1,0:T(8,128)(2,1)} %param.9) | copy-start | bytes 1966084
  0.7 0.8 copy-start.4
  1.5 0.7 copy-start.5
  2.2 30.4 %copy-start.6 = (f32[40]{0:T(128)S(1)}, f32[40]{0:T(128)}, u32[]{:S(2)}) copy-start(f32[40]{0:T(128)} %param.14) | copy-start | bytes 484
  2.2 30.4 %copy-start.7 = (f32[40]{0:T(128)S(1)}, f32[40]{0:T(128)}, u32[]{:S(2)}) copy-start(f32[40]{0:T(128)} %param.13) | copy-start | bytes 484
  26.6 6.0 %collective-permute-start = (bf16[32,56,128]{2,1,0:T(8,128)(2,1)S(1)}, bf16[32,56,128]{2,1,0:T(8,128)(2,1)S(1)}, u32[]{:S(2)}, u32[]{:S(2)}) collective-permute-start(bf16[32,56,128]{2,1,0:T(8,128)(2,1)S(1)} %all_to_all.20.mine_ref), channel_id=1, source_target_pairs={{0,1},{1,0},{2,3},{3,2},{4,5},{5,4},{6,7},{7,6},{8,9},{9,8},{10,11... | collective-permute-start | bytes 1376264 | tf_op jit(solution)/shard_map/ppermute | solution.py:459
  68.9 5.1 %copy-start.2 = (bf16[1,128,2560]{2,1,0:T(8,128)(2,1)S(1)}, bf16[1,128,2560]{2,1,0:T(8,128)(2,1)}, u32[]{:S(2)}) copy-start(bf16[1,128,2560]{2,1,0:T(8,128)(2,1)} %param.8) | copy-start | bytes 1966084
  70.3 21.7 %all-to-all-start.2 = ((bf16[16,160,128]{2,1,0:T(8,128)(2,1)}), bf16[16,160,128]{2,1,0:T(8,128)(2,1)S(1)}, u32[]{:S(2)}, u32[]{:S(2)}) async-start(bf16[16,160,128]{2,1,0:T(8,128)(2,1)} %chain.1), calls=%async_computation.2 | async-start | bytes 1310720 | tf_op jit(solution)/shard_map/all_to_all | solution.py:476
  74.0 18.0 %copy-start.8 = (f32[40]{0:T(128)S(1)}, f32[40]{0:T(128)}, u32[]{:S(2)}) copy-start(f32[40]{0:T(128)} %param.15) | copy-start | bytes 484
  92.1 8.6 %copy-start.3 = (bf16[2560,256]{1,0:T(8,128)(2,1)S(1)}, bf16[2560,256]{1,0:T(8,128)(2,1)}, u32[]{:S(2)}) copy-start(bf16[2560,256]{1,0:T(8,128)(2,1)} %get-tuple-element.22.weight_ref) | copy-start | bytes 3932164
  98.6 3.7 %collective-permute-start.1 = (bf16[32,56,128]{2,1,0:T(8,128)(2,1)S(1)}, bf16[32,56,128]{2,1,0:T(8,128)(2,1)S(1)}, u32[]{:S(2)}, u32[]{:S(2)}) collective-permute-start(bf16[32,56,128]{2,1,0:T(8,128)(2,1)S(1)} %get-tuple-element.26), channel_id=1, source_target_pairs={{0,1},{1,0},{2,3},{3,2},{4,5},{5,4},{6,7},{7,6},{8,9},{9,8},{10,11... | collective-permute-start | bytes 1376264 | tf_op jit(solution)/shard_map/ppermute | solution.py:509

commit v4 on v3

--- a/solution.py
+++ b/solution.py
@@ -17,6 +17,8 @@
 ROWS = 80
 DP = 32
 SEQ = 16
+CHIPS = 8
+STATE = 64
 HALF = 56
 REST = 24
 LANES = 128
@@ -49,13 +51,6 @@
 
 def head_of_lane(lane):
     return lane - jnp.where(lane >= 40, 40, 0) - jnp.where(lane >= 80, 40, 0)
-
-
-def interleave(shape, source_axis):
-    source, target = iota(shape, source_axis), iota(shape, 1 - source_axis)
-    low = target & 7
-    wanted = 4 * (target >> 3) + low + jnp.where(low >= 4, 60, 0)
-    return ones_where(source == wanted)
 
 
 def triple(row):
@@ -83,7 +78,7 @@
 
 
 def pack_kernel(core_ref, bc_ref, dt_ref, out_ref):
-    bc = mm(bc_ref[...], interleave((LANES, LANES), 0))
+    bc = bc_ref[...].astype(f32)
     row, lane = iota((HEADS, LANES), 0), iota((HEADS, LANES), 1)
     dt = [mm(dt_ref[...], ones_where(lane == row + 40 * k), TN) for k in range(3)]
     last = jnp.concatenate([dt[2][64:80], jnp.zeros((16, LANES), f32)], axis=0)
@@ -102,7 +97,7 @@
 
 def first_kernel(
     core_ref, mine_ref, other_ref, feat_hbm, x_ref, g_ref, bias_ref, rate_ref,
-    weight_hbm, small_ref, state_ref, weight_ref, feat_ref, sems,
+    weight_hbm, small_ref, held_ref, sent_ref, weight_ref, feat_ref, sems,
 ):
     fetch = pltpu.make_async_copy(feat_hbm, feat_ref, sems.at[0])
     fetch.start()
@@ -152,80 +147,102 @@
         [split(step * jnp.exp(total - cum)), split(jnp.exp(cum))], axis=0
     )
     turned_high, turned_low = high_low(proj.T)
-    both_turned = jnp.concatenate([turned_high, turned_low], axis=0)
-    forward = (iota((LANES, 2 * LANES), 0) & 7) < 4
+    b_turned = jnp.concatenate([turned_high[0:STATE], turned_low[0:STATE]], axis=0)
+    c_turned = jnp.concatenate([turned_high[STATE:], turned_low[STATE:]], axis=0)
+
+    def product(turned, halves):
+        value = mm(turned, halves[0])
+        return value[0:STATE] + (value[STATE:] + mm(turned[0:STATE], halves[1]))
 
     for two in range(PAIRS // 2):
         cols = slice(256 * two, 256 * two + 256)
+        rows = slice(16 * two, 16 * two + 16)
         wide = lax.dot_general(
             stacked, spread_matrix(2 * two, 2), NN, preferred_element_type=f32
         )
-        ending = high_low(x_ref[:, cols].astype(f32) * wide[0:TOK])
-        weighted = high_low(g_ref[:, cols].astype(f32) * wide[TOK:])
-
-        def product(halves):
-            value = mm(both_turned, halves[0])
-            return value[0:LANES] + (value[LANES:] + mm(turned_high, halves[1]))
-
-        chosen = jnp.where(forward, product(ending), product(weighted))
-        value = jnp.concatenate(
-            [chosen[:, k * LANES : k * LANES + LANES].reshape(SEQ, 8, LANES) for k in range(2)],
-            axis=1,
-        )
-        state_ref[:, 16 * two : 16 * two + 16, :] = value.astype(bf16)
-    decay = split(jnp.broadcast_to(total, (8, LANES)))
-    for owner in range(SEQ):
-        state_ref[owner, 160:168, :] = decay
+        onward = product(b_turned, high_low(x_ref[:, cols].astype(f32) * wide[0:TOK]))
+        backward = product(c_turned, high_low(g_ref[:, cols].astype(f32) * wide[TOK:]))
+        held_ref[:, rows, :] = to_chunks(jnp.where(core == 0, onward, backward))
+        sent_ref[:, rows, :] = to_chunks(jnp.where(core == 0, backward, onward))
+    for owner in range(CHIPS):
+        sent_ref[owner, 160:168, :] = jnp.broadcast_to(total, (8, LANES))
     store.wait()
 
 
-def chain_kernel(state_ref, out_ref):
+def to_chunks(value):
+    parts = [value[:, LANES * k : LANES * k + LANES] for k in range(2)]
+    return jnp.concatenate([part.reshape(CHIPS, 8, LANES) for part in parts], axis=1)
+
+
+def chunk_factors(logs, two):
+    wide = jnp.exp(
+        lax.dot_general(logs, spread_matrix(2 * two, 2), NN, preferred_element_type=f32)
+    )
+
+    def factor(place):
+        parts = [wide[place : place + 1, LANES * k : LANES * k + LANES] for k in range(2)]
+        return jnp.concatenate([jnp.broadcast_to(part, (8, LANES)) for part in parts], axis=0)
+
+    return factor
+
+
+def chip_kernel(held_ref, other_ref, small_ref, out_ref):
+    total_other = other_ref[0, 160:168, :]
+    logs = split(jnp.concatenate([total_other, total_other], axis=0))
+    for two in range(PAIRS // 2):
+        rows = slice(16 * two, 16 * two + 16)
+        factor = chunk_factors(logs, two)(0)
+        for owner in range(CHIPS):
+            value = other_ref[owner, rows, :] + held_ref[owner, rows, :] * factor
+            out_ref[owner, rows, :] = value.astype(bf16)
+    decay = split(total_other + small_ref[2, TOK - 1 : TOK, :])
+    for owner in range(CHIPS):
+        out_ref[owner, 160:168, :] = decay
+
+
+def chain_kernel(core_ref, state_ref, out_ref):
     row16 = iota((16, LANES), 0)
     logs = jnp.zeros((16, LANES), f32)
-    for place in range(SEQ):
+    for place in range(CHIPS):
         line = state_ref[place, 160:168, :].astype(f32)
         logs = logs + jnp.where(row16 == place, jnp.concatenate([line, line], axis=0), 0.0)
     logs = logs.astype(bf16)
-    forward = (row16 & 7) < 4
+    forward = core_ref[0] == 0
     for two in range(PAIRS // 2):
         rows = slice(16 * two, 16 * two + 16)
-        factor = [
-            jnp.exp(
-                lax.dot_general(
-                    logs, spread_matrix(2 * two + k), NN, preferred_element_type=f32
-                )
-            )
-            for k in range(2)
-        ]
-
-        def decay(place):
-            return jnp.concatenate(
-                [jnp.broadcast_to(factor[k][place : place + 1], (8, LANES)) for k in range(2)],
-                axis=0,
-            )
-
-        values = [state_ref[place, rows, :].astype(f32) for place in range(SEQ)]
-        decays = [decay(place) for place in range(SEQ)]
+        factor = chunk_factors(logs, two)
+        values = [state_ref[place, rows, :].astype(f32) for place in range(CHIPS)]
+        factors = [factor(place) for place in range(CHIPS)]
         ahead = [jnp.zeros((16, LANES), f32)]
-        for place in range(SEQ - 1):
-            ahead.append(ahead[-1] * decays[place] + values[place])
+        for place in range(CHIPS - 1):
+            ahead.append(ahead[-1] * factors[place] + values[place])
         back = jnp.zeros((16, LANES), f32)
-        for place in range(SEQ - 1, -1, -1):
+        for place in range(CHIPS - 1, -1, -1):
             out_ref[place, rows, :] = jnp.where(forward, ahead[place], back).astype(bf16)
-            back = back * decays[place] + values[place]
+            back = back * factors[place] + values[place]
+
+
+def pass_kernel(carried_ref, held_ref, small_ref, after_ref, out_ref):
+    logs = split(jnp.broadcast_to(small_ref[2, TOK - 1 : TOK, :], (16, LANES)))
+    for two in range(PAIRS // 2):
+        rows = slice(16 * two, 16 * two + 16)
+        factor = chunk_factors(logs, two)(0)
+        for owner in range(CHIPS):
+            value = carried_ref[owner, rows, :].astype(f32) * factor + held_ref[owner, rows, :]
+            out_ref[owner, rows, :] = value.astype(bf16)
 
 
 def softplus(pre):
     return jnp.maximum(pre, 0.0) + jnp.log1p(jnp.exp(-jnp.abs(pre)))
 
 
-def inside_kernel(small_ref, x_ref, g_ref, scaled_hbm, sums_ref, scaled_ref, sem):
+def inside_kernel(small_ref, x_ref, g_ref, after_ref, scaled_hbm, sums_ref, scaled_ref, sem):
     proj, cum = small_ref[0], small_ref[2]
     step = softplus(small_ref[1])
     row, lane = iota((LANES, LANES), 0), iota((LANES, LANES), 1)
-    low = (lane & 7) < 4
+    low = lane < STATE
     b_low = jnp.where(low, proj, 0.0)
-    c_low = jnp.where(low, pltpu.roll(proj, LANES - 4, 1), 0.0)
+    c_low = jnp.where(low, pltpu.roll(proj, STATE, 1), 0.0)
     meet = mm_exact(b_low, c_low, NT)
     causal = lane >= row
     cum_turned = cum.T
@@ -265,7 +282,7 @@
 
 
 def last_kernel(
-    core_ref, carried_ref, small_ref, scaled_hbm, inner_ref, turned_ref, x_ref, g_ref,
+    core_ref, carried_ref, other_ref, small_ref, scaled_hbm, inner_ref, turned_ref, x_ref, g_ref,
     rate_ref, skip_ref,
     grads_ref, head_grad_ref, keep_ref, send_ref,
     scaled_ref, state_all, lines_all, terms_all, select_all, sem,
@@ -276,9 +293,11 @@
     step = softplus(pre)
     total = cum[TOK - 1 : TOK]
     row, lane = iota((LANES, LANES), 0), iota((LANES, LANES), 1)
-    low = (lane & 7) < 4
-    c_low = jnp.where(low, pltpu.roll(proj, LANES - 4, 1), 0.0)
-    b_high = jnp.where(low, 0.0, pltpu.roll(proj, 4, 1))
+    low = lane < STATE
+    proj_swapped = pltpu.roll(proj, STATE, 1)
+    c_low = jnp.where(low, proj_swapped, 0.0)
+    b_high = jnp.where(low, 0.0, proj_swapped)
+    first_core = core_ref[0] == 0
     left = jnp.concatenate([c_low, b_high], axis=0)
     left = jnp.concatenate(high_low(left), axis=0)
     stacked = jnp.concatenate(
@@ -290,15 +309,20 @@
         ],
         axis=0,
     )
-    low_rows = (iota((LANES, 2 * LANES), 0) & 7) < 4
+
+    def state_rows(chunk):
+        parts = [chunk[:, 8 * k : 8 * k + 8, :].reshape(STATE, LANES) for k in range(2)]
+        return jnp.concatenate(parts, axis=1)
+
     for two in range(PAIRS // 2):
         cols = slice(256 * two, 256 * two + 256)
         later_cols = slice(WIDE + 256 * two, WIDE + 256 * two + 256)
-        chunk = carried_ref[:, 16 * two : 16 * two + 16, :].astype(f32)
-        state = jnp.concatenate(
-            [chunk[:, 8 * k : 8 * k + 8, :].reshape(LANES, LANES) for k in range(2)], axis=1
-        )
-        state_b = state.astype(bf16)
+        rows = slice(16 * two, 16 * two + 16)
+        mine = carried_ref[:, rows, :].astype(f32)
+        other = other_ref[:, rows, :].astype(f32)
+        state_in = state_rows(jnp.where(first_core, mine, other))
+        state_grad = state_rows(jnp.where(first_core, other, mine))
+        state_b = jnp.concatenate([state_in, state_grad], axis=0).astype(bf16)
         state_all[:, cols] = state_b
         select_all[cols, :] = gather_matrix(2 * two, 2)
         wide = lax.dot_general(
@@ -315,8 +339,7 @@
         high, low_part = high_low(jnp.concatenate([weighted, ending * step_w], axis=0))
         lines_all[:, cols] = high
         lines_all[:, later_cols] = low_part
-        pairing = jnp.where(low_rows, state * pltpu.roll(state, LANES - 4, 0), 0.0)
-        pairing = jnp.sum(pairing.reshape(SEQ, 8, 2 * LANES), axis=0)
+        pairing = jnp.sum((state_in * state_grad).reshape(CHIPS, 8, 2 * LANES), axis=0)
         pairing = jnp.concatenate([pairing, jnp.zeros((8, 2 * LANES), f32)], axis=0)
         high, low_part = high_low(
             jnp.concatenate([weighted * out, ending * reach, pairing], axis=0)
@@ -351,12 +374,11 @@
     across = inner_ref[0]
     bc_grad = mm_exact(across, c_low) + mm_exact(across.T, b_high)
     bc_grad = bc_grad + jnp.where(
-        low, pltpu.roll(crossed[TOK:], LANES - 4, 1), pltpu.roll(crossed[0:TOK], 4, 1)
+        low, pltpu.roll(crossed[TOK:], STATE, 1), pltpu.roll(crossed[0:TOK], STATE, 1)
     )
     grads = high_low(jnp.concatenate([bc_grad, pre_grad], axis=1))
     tall, flat = jnp.concatenate(grads, axis=0), jnp.concatenate(grads, axis=1)
     grads_ref[...] = tall
-    first_core = core_ref[0] == 0
     lane32 = iota((32, LANES), 1)
     zeros = jnp.zeros((16, LANES), f32)
     for part in range(4):
@@ -400,7 +422,7 @@
         two = two + parts_ref[place + 1].astype(f32)
     scale = 1.0 / math.sqrt(SEQ * DP * TOK)
     bc = jnp.concatenate([one, two[0:REST]], axis=0) * scale
-    bc_ref[...] = mm_exact(bc, interleave((LANES, LANES), 1))
+    bc_ref[...] = bc
     packed = two[REST:HALF] * scale
     head, lane = iota((HEADS, LANES), 0), iota((HEADS, LANES), 1)
     for k in range(3):
@@ -410,7 +432,7 @@
         )
 
 
-def call(kernel, name, out_shape, scalars, arrays, in_hbm=(), out_hbm=(), **options):
+def call(kernel, name, out_shape, scalars, arrays, in_hbm=(), out_hbm=(), after=(), **options):
     smem = pl.BlockSpec(memory_space=pltpu.SMEM)
     vmem = pl.BlockSpec(memory_space=pltpu.VMEM)
     hbm = pl.BlockSpec(memory_space=pltpu.HBM)
@@ -431,12 +453,13 @@
         name=name,
         out_shape=out_shape,
         in_specs=[smem] * len(scalars)
-        + [hbm if k in in_hbm else vmem for k in range(len(arrays))],
+        + [hbm if k in in_hbm else vmem for k in range(len(arrays))]
+        + [pl.BlockSpec(memory_space=pl.ANY)] * len(after),
         out_specs=tuple(out_specs) if several else out_specs,
         scratch_shapes=options.pop("scratch", ()),
         compiler_params=pltpu.CompilerParams(vmem_limit_bytes=40 << 20),
         cost_estimate=pl.CostEstimate(flops=flops, bytes_accessed=moved, transcendentals=0),
-    )(*scalars, *arrays)
+    )(*scalars, *arrays, *after)
 
 
 def shape(dims, dtype):
@@ -444,6 +467,11 @@
 
 
 SWAP = [(place, place ^ 1) for place in range(SEQ)]
+CORES = [[place for place in range(SEQ) if place % 2 == core] for core in range(2)]
+
+
+def same_core_all_to_all(value):
+    return lax.all_to_all(value, "seq", 0, 0, axis_index_groups=CORES, tiled=True)
 
 
 def body(features, head_inputs, out_grad, bc_weight, dt_weight, dt_bias, decay_rate, skip_gain):
@@ -457,10 +485,15 @@
     sent = call(pack_kernel, "pack", chunks, [core], [bc_weight, dt_weight.T])
     mine = lax.all_to_all(sent, "dp", 0, 0, tiled=True)
     other = lax.ppermute(mine, "seq", SWAP)
-    weight, small, local = call(
+    weight, small, held, leaving = call(
         first_kernel,
         "first",
-        (shape((WIDE, 2 * LANES), bf16), three, shape((SEQ, 168, LANES), bf16)),
+        (
+            shape((WIDE, 2 * LANES), bf16),
+            three,
+            shape((CHIPS, 160, LANES), f32),
+            shape((CHIPS, 168, LANES), f32),
+        ),
         [core],
         [mine, other, feats, x, g, bias, rate],
         in_hbm=(2,),
@@ -471,9 +504,12 @@
             dma((2,)),
         ],
     )
-    gathered = lax.all_to_all(local, "seq", 0, 0, tiled=True)
-    entering = call(chain_kernel, "chain", shape((SEQ, 160, LANES), bf16), [], [gathered])
-    carried = lax.all_to_all(entering, "seq", 0, 0, tiled=True)
+    other = lax.ppermute(leaving, "seq", SWAP)
+    local = call(chip_kernel, "chip", shape((CHIPS, 168, LANES), bf16), [], [held, other, small])
+    gathered = same_core_all_to_all(local)
+    states = shape((CHIPS, 160, LANES), bf16)
+    entering = call(chain_kernel, "chain", states, [core], [gathered])
+    carried = same_core_all_to_all(entering)
     scaled, inner = call(
         inside_kernel,
         "inside",
@@ -481,9 +517,12 @@
         [],
         [small, x, g],
         out_hbm=(0,),
+        after=[entering],
         scratch=[pltpu.VMEM((TOK, WIDE), f32), dma],
         cost=(400_000_000, 4_000_000),
     )
+    passed = call(pass_kernel, "pass", states, [], [carried, held, small], after=[inner])
+    other_carried = lax.ppermute(passed, "seq", SWAP)
     turned = call(turn_kernel, "turn", shape((WIDE, TOK), bf16), [], [feats], cost=(0, 2_000_000))
     grads, head_grad, keep, send = call(
         last_kernel,
@@ -495,8 +534,8 @@
             chunks,
         ),
         [core],
-        [carried, small, scaled, inner, turned, x, g, rate, skip],
-        in_hbm=(2,),
+        [carried, other_carried, small, scaled, inner, turned, x, g, rate, skip],
+        in_hbm=(3,),
         scratch=[
             pltpu.VMEM((TOK, WIDE), f32),
             pltpu.VMEM((LANES, WIDE), bf16),

time: 142 us -> 135 us (0.951)
  blocking collectives: 93.4 us -> 84.5 us
  starting transfers between devices: 10.3 us -> 17.8 us
  waiting for transfers between devices: 13.9 us -> 9.42 us
    all_to_all x1, blocking collectives: 31.4 us -> 22.9 us  [same_core_all_to_all(): lax.all_to_all(value, 'seq', 0, 0, axis_index_groups=CORES, tiled=True)]
    ppermute x0 -> x2, starting transfers between devices: none -> 7.48 us  [the longest x1 5.19 us: body(): other_carried = lax.ppermute(passed, 'seq', SWAP)]
    all_to_all x1, waiting for transfers between devices: 12.2 us -> 5.4 us  [same_core_all_to_all(): lax.all_to_all(value, 'seq', 0, 0, axis_index_groups=CORES, tiled=True)]
    ppermute x0 -> x2, waiting for transfers between devices: none -> 2.57 us  [the longest x1 1.75 us: body(): other = lax.ppermute(leaving, 'seq', SWAP)]
    pallas_call x9 -> x11, Pallas kernels: 21.4 us -> 20.6 us  [call(): pl.pallas_call(kernel, name=name, out_shape=out_shape, in_specs=[smem] *...]
  transfers between devices with their start and end apart: 3 -> 5, of which waited for: 3 -> 4; matrix products, arithmetic and copies ran while one was open for 0% -> 0% of each run, Pallas kernels for 5% -> 5%
where the time goes in v4:
time: 135 us
  blocking collectives  84.5 us (63%)
  Pallas kernels  20.6 us (15%)
  starting transfers between devices  17.8 us (13%)
  waiting for transfers between devices  9.42 us (7%)
  local copies, waits for them, and re-layouts  1.55 us (1%)
    all_to_all x1, blocking collectives, body(): mine = lax.all_to_all(sent, 'dp', 0, 0, tiled=True)  24.1 us
    all_to_all x1, blocking collectives, same_core_all_to_all(): lax.all_to_all(value, 'seq', 0, 0, axis_index_groups=CORES, tiled=True)  22.9 us
    pallas_call x11, Pallas kernels, call(): pl.pallas_call(kernel, name=name, out_shape=out_shape, in_specs=[smem] *...  20.6 us
    all_to_all x1, blocking collectives, body(): owned = lax.all_to_all(paired, 'dp', 0, 0, tiled=True)  19.2 us
    all_gather x1, blocking collectives, body(): parts = lax.all_gather(owned, 'seq')  18.3 us
    all_to_all x1, waiting for transfers between devices, same_core_all_to_all(): lax.all_to_all(value, 'seq', 0, 0, axis_index_groups=CORES, tiled=True)  5.4 us
    ppermute x1, starting transfers between devices, body(): other_carried = lax.ppermute(passed, 'seq', SWAP)  5.19 us
    ppermute x1, starting transfers between devices, body(): other = lax.ppermute(mine, 'seq', SWAP)  4.59 us
  transfers between devices with their start and end apart: 5, of which 4 were waited for; matrix products, arithmetic and copies ran while one was open for 0% of the time, Pallas kernels for 5%

profile of v4, /device:TPU:9, one launch (start us, length us, event | category | flops | bytes accessed | tf_op | source)
XLA Modules:
  0.0 134.7 jit_solution(14963111794356951364)
XLA Ops:
  0.7 0.8 copy-done.4
  1.5 0.7 copy-done.5
  2.4 24.1 %all_to_all.20.mine_ref = bf16[32,56,128]{2,1,0:T(8,128)(2,1)S(1)} all-to-all(bf16[32,56,128]{2,1,0:T(8,128)(2,1)S(1)} %pack.1), channel_id=1, replica_groups=mesh['dp'=32,'seq'=16] {'dp'}, dimensions={0} | all-to-all | bytes 917504 | tf_op jit(solution)/shard_map/all_to_all | solution.py:486
  26.6 4.6 %collective-permute-start = (bf16[32,56,128]{2,1,0:T(8,128)(2,1)S(1)}, bf16[32,56,128]{2,1,0:T(8,128)(2,1)S(1)}, u32[]{:S(2)}, u32[]{:S(2)}) collective-permute-start(bf16[32,56,128]{2,1,0:T(8,128)(2,1)S(1)} %all_to_all.20.mine_ref), channel_id=1, source_target_pairs={{0,1},{1,0},{2,3},{3,2},{4,5},{5,4},{6,7},{7,6},{8,9},{9,8},{10,11... | collective-permute-start | bytes 1376264 | tf_op jit(solution)/shard_map/ppermute | solution.py:487
  31.2 1.4 %collective-permute-done.other_ref = bf16[32,56,128]{2,1,0:T(8,128)(2,1)S(1)} collective-permute-done((bf16[32,56,128]{2,1,0:T(8,128)(2,1)S(1)}, bf16[32,56,128]{2,1,0:T(8,128)(2,1)S(1)}, u32[]{:S(2)}, u32[]{:S(2)}) %collective-permute-start) | collective-permute-done | bytes 458784 | tf_op jit(solution)/shard_map/ppermute | solution.py:487
  32.6 4.2 %first.1 = (bf16[2560,256]{1,0:T(8,128)(2,1)}, f32[3,128,128]{2,1,0:T(8,128)S(1)}, f32[8,160,128]{2,1,0:T(8,128)S(1)}, f32[8,168,128]{2,1,0:T(8,128)S(1)}) custom-call(s32[1]{0:T(128)} %bitcast.core_ref, bf16[32,56,128]{2,1,0:T(8,128)(2,1)S(1)} %all_to_all.20.mine_ref, bf16[32,56,128]{2,1,0:T(8,128)(2,1)S(1)} %collective-permute-done.other_ref, ...), custom_call_target="tpu_custom_call" | custom-call | tf_op jit(solution)/shard_map/first/pallas_call | solution.py:451
  36.8 2.3 %collective-permute-start.1 = (f32[8,168,128]{2,1,0:T(8,128)S(1)}, f32[8,168,128]{2,1,0:T(8,128)S(1)}, u32[]{:S(2)}, u32[]{:S(2)}) collective-permute-start(f32[8,168,128]{2,1,0:T(8,128)S(1)} %get-tuple-element.19), channel_id=1, source_target_pairs={{0,1},{1,0},{2,3},{3,2},{4,5},{5,4},{6,7},{7,6},{8,9},{9,8},{10,11... | collective-permute-start | bytes 2064392 | tf_op jit(solution)/shard_map/ppermute | solution.py:507
  39.1 1.7 %collective-permute-done.1.other_ref = f32[8,168,128]{2,1,0:T(8,128)S(1)} collective-permute-done((f32[8,168,128]{2,1,0:T(8,128)S(1)}, f32[8,168,128]{2,1,0:T(8,128)S(1)}, u32[]{:S(2)}, u32[]{:S(2)}) %collective-permute-start.1) | collective-permute-done | bytes 688160 | tf_op jit(solution)/shard_map/ppermute | solution.py:507
  40.9 0.2 chip.1
  41.1 22.9 %all_to_all.21.state_ref = bf16[8,168,128]{2,1,0:T(8,128)(2,1)S(1)} all-to-all(bf16[8,168,128]{2,1,0:T(8,128)(2,1)S(1)} %chip.1), channel_id=1, replica_groups={{0,2,4,6,8,10,12,14},{1,3,5,7,9,11,13,15},{16,18,20,22,24,26,28,30},{17..., dimensions={0} | all-to-all | bytes 688128 | tf_op jit(solution)/shard_map/all_to_all | solution.py:474
  64.0 1.1 chain.1.after_ref
  65.0 3.4 %all-to-all-start.2 = ((bf16[8,160,128]{2,1,0:T(8,128)(2,1)}), bf16[8,160,128]{2,1,0:T(8,128)(2,1)S(1)}, u32[]{:S(2)}, u32[]{:S(2)}) async-start(bf16[8,160,128]{2,1,0:T(8,128)(2,1)} %chain.1.after_ref), calls=%async_computation.2 | async-start | bytes 655360 | tf_op jit(solution)/shard_map/all_to_all | solution.py:474
  68.5 5.6 %inside.1 = (f32[128,2560]{1,0:T(8,128)}, f32[3,128,128]{2,1,0:T(8,128)S(1)}) custom-call(f32[3,128,128]{2,1,0:T(8,128)S(1)} %get-tuple-element.20.small_ref, bf16[128,2560]{1,0:T(8,128)(2,1)S(1)} %bitcast.13, bf16[128,2560]{1,0:T(8,128)(2,1)S(1)} %bitcast.16, bf16[8,160,128]{2,1,0:T(8,128)(2,1)} %chain.1.after_ref), custom_call_target="tpu_custom_call" | custom-call | flops 400000000 | bytes 4000000 | tf_op jit(solution)/shard_map/inside/pallas_call | solution.py:451
  74.1 5.4 %all-to-all-done.2.carried_ref = bf16[8,160,128]{2,1,0:T(8,128)(2,1)S(1)} async-done(((bf16[8,160,128]{2,1,0:T(8,128)(2,1)}), bf16[8,160,128]{2,1,0:T(8,128)(2,1)S(1)}, u32[]{:S(2)}, u32[]{:S(2)}) %all-to-all-start.2) | async-done | bytes 327712 | tf_op jit(solution)/shard_map/all_to_all | solution.py:474
  79.5 0.2 pass.1
  79.8 5.2 %collective-permute-start.2 = (bf16[8,160,128]{2,1,0:T(8,128)(2,1)S(1)}, bf16[8,160,128]{2,1,0:T(8,128)(2,1)S(1)}, u32[]{:S(2)}, u32[]{:S(2)}) collective-permute-start(bf16[8,160,128]{2,1,0:T(8,128)(2,1)S(1)} %pass.1), channel_id=1, source_target_pairs={{0,1},{1,0},{2,3},{3,2},{4,5},{5,4},{6,7},{7,6},{8,9},{9,8},{10,11... | collective-permute-start | bytes 983048 | tf_op jit(solution)/shard_map/ppermute | solution.py:525
  85.0 0.2 turn.1.turned_ref
  85.2 0.8 collective-permute-done.2.other_ref
  86.0 6.4 %last.1 = (bf16[256,256]{1,0:T(8,128)(2,1)S(1)}, bf16[128,2560]{1,0:T(8,128)(2,1)}, f32[32,56,128]{2,1,0:T(8,128)S(1)}, bf16[32,56,128]{2,1,0:T(8,128)(2,1)S(1)}) custom-call(s32[1]{0:T(128)} %bitcast.core_ref, bf16[8,160,128]{2,1,0:T(8,128)(2,1)S(1)} %all-to-all-done.2.carried_ref, bf16[8,160,128]{2,1,0:T(8,128)(2,1)S(1)} %collective-permute-done.2.other_ref, ...), custom_call_target="tpu_custom_call" | custom-call | tf_op jit(solution)/shard_map/last/pallas_call | solution.py:451
  92.5 2.3 %collective-permute-start.3 = (bf16[32,56,128]{2,1,0:T(8,128)(2,1)S(1)}, bf16[32,56,128]{2,1,0:T(8,128)(2,1)S(1)}, u32[]{:S(2)}, u32[]{:S(2)}) collective-permute-start(bf16[32,56,128]{2,1,0:T(8,128)(2,1)S(1)} %get-tuple-element.28), channel_id=1, source_target_pairs={{0,1},{1,0},{2,3},{3,2},{4,5},{5,4},{6,7},{7,6},{8,9},{9,8},{10,11... | collective-permute-start | bytes 1376264 | tf_op jit(solution)/shard_map/ppermute | solution.py:548
  94.8 1.4 %back.1 = (bf16[128,2560]{1,0:T(8,128)(2,1)}, f32[8,128]{1,0:T(8,128)S(1)}) custom-call(bf16[256,256]{1,0:T(8,128)(2,1)S(1)} %get-tuple-element.23.grads_ref, bf16[2560,256]{1,0:T(8,128)(2,1)S(1)} %copy-done.3), custom_call_target="tpu_custom_call" | custom-call | flops 340000000 | bytes 3000000 | tf_op jit(solution)/shard_map/back/pallas_call | solution.py:451
  96.3 19.2 %all_to_all.22 = bf16[32,56,128]{2,1,0:T(8,128)(2,1)S(1)} all-to-all(bf16[32,56,128]{2,1,0:T(8,128)(2,1)S(1)} %join.1), channel_id=1, replica_groups=mesh['dp'=32,'seq'=16] {'dp'}, dimensions={0} | all-to-all | bytes 917504 | tf_op jit(solution)/shard_map/all_to_all | solution.py:558
  115.5 18.3 %all-gather = f32[896,128]{1,0:T(8,128)S(1)} all-gather(f32[56,128]{1,0:T(8,128)S(1)} %convert_reduce_fusion), channel_id=2, replica_groups=mesh['dp'=32,'seq'=16] {'seq'}, dimensions={0}, use_global_device_ids=true | all-gather | bytes 487424 | tf_op jit(solution)/shard_map/all_gather | solution.py:560
  133.8 0.9 finish.1
  (20 shorter events, 0.4 us)
Async XLA Ops:
  0.6 32.0 %copy-start.1 = (bf16[1,128,2560]{2,1,0:T(8,128)(2,1)S(1)}, bf16[1,128,2560]{2,1,0:T(8,128)(2,1)}, u32[]{:S(2)}) copy-start(bf16[1,128,2560]{2,1,0:T(8,128)(2,1)} %param.10) | copy-start | bytes 1966084
  0.6 31.9 %copy-start = (bf16[1,128,2560]{2,1,0:T(8,128)(2,1)S(1)}, bf16[1,128,2560]{2,1,0:T(8,128)(2,1)}, u32[]{:S(2)}) copy-start(bf16[1,128,2560]{2,1,0:T(8,128)(2,1)} %param.9) | copy-start | bytes 1966084
  0.7 0.8 copy-start.4
  1.5 0.7 copy-start.5
  2.2 30.4 %copy-start.6 = (f32[40]{0:T(128)S(1)}, f32[40]{0:T(128)}, u32[]{:S(2)}) copy-start(f32[40]{0:T(128)} %param.14) | copy-start | bytes 484
  2.2 30.4 %copy-start.7 = (f32[40]{0:T(128)S(1)}, f32[40]{0:T(128)}, u32[]{:S(2)}) copy-start(f32[40]{0:T(128)} %param.13) | copy-start | bytes 484
  26.6 6.0 %collective-permute-start = (bf16[32,56,128]{2,1,0:T(8,128)(2,1)S(1)}, bf16[32,56,128]{2,1,0:T(8,128)(2,1)S(1)}, u32[]{:S(2)}, u32[]{:S(2)}) collective-permute-start(bf16[32,56,128]{2,1,0:T(8,128)(2,1)S(1)} %all_to_all.20.mine_ref), channel_id=1, source_target_pairs={{0,1},{1,0},{2,3},{3,2},{4,5},{5,4},{6,7},{7,6},{8,9},{9,8},{10,11... | collective-permute-start | bytes 1376264 | tf_op jit(solution)/shard_map/ppermute | solution.py:487
  36.8 4.0 %collective-permute-start.1 = (f32[8,168,128]{2,1,0:T(8,128)S(1)}, f32[8,168,128]{2,1,0:T(8,128)S(1)}, u32[]{:S(2)}, u32[]{:S(2)}) collective-permute-start(f32[8,168,128]{2,1,0:T(8,128)S(1)} %get-tuple-element.19), channel_id=1, source_target_pairs={{0,1},{1,0},{2,3},{3,2},{4,5},{5,4},{6,7},{7,6},{8,9},{9,8},{10,11... | collective-permute-start | bytes 2064392 | tf_op jit(solution)/shard_map/ppermute | solution.py:507
  65.0 14.5 %all-to-all-start.2 = ((bf16[8,160,128]{2,1,0:T(8,128)(2,1)}), bf16[8,160,128]{2,1,0:T(8,128)(2,1)S(1)}, u32[]{:S(2)}, u32[]{:S(2)}) async-start(bf16[8,160,128]{2,1,0:T(8,128)(2,1)} %chain.1.after_ref), calls=%async_computation.2 | async-start | bytes 655360 | tf_op jit(solution)/shard_map/all_to_all | solution.py:474
  74.1 10.9 %copy-start.2 = (bf16[1,128,2560]{2,1,0:T(8,128)(2,1)S(1)}, bf16[1,128,2560]{2,1,0:T(8,128)(2,1)}, u32[]{:S(2)}) copy-start(bf16[1,128,2560]{2,1,0:T(8,128)(2,1)} %param.8) | copy-start | bytes 1966084
  79.5 6.5 %copy-start.8 = (f32[40]{0:T(128)S(1)}, f32[40]{0:T(128)}, u32[]{:S(2)}) copy-start(f32[40]{0:T(128)} %param.15) | copy-start | bytes 484
  79.8 6.3 %collective-permute-start.2 = (bf16[8,160,128]{2,1,0:T(8,128)(2,1)S(1)}, bf16[8,160,128]{2,1,0:T(8,128)(2,1)S(1)}, u32[]{:S(2)}, u32[]{:S(2)}) collective-permute-start(bf16[8,160,128]{2,1,0:T(8,128)(2,1)S(1)} %pass.1), channel_id=1, source_target_pairs={{0,1},{1,0},{2,3},{3,2},{4,5},{5,4},{6,7},{7,6},{8,9},{9,8},{10,11... | collective-permute-start | bytes 983048 | tf_op jit(solution)/shard_map/ppermute | solution.py:525
  86.0 8.7 %copy-start.3 = (bf16[2560,256]{1,0:T(8,128)(2,1)S(1)}, bf16[2560,256]{1,0:T(8,128)(2,1)}, u32[]{:S(2)}) copy-start(bf16[2560,256]{1,0:T(8,128)(2,1)} %get-tuple-element.24.weight_ref) | copy-start | bytes 3932164
  92.5 3.7 %collective-permute-start.3 = (bf16[32,56,128]{2,1,0:T(8,128)(2,1)S(1)}, bf16[32,56,128]{2,1,0:T(8,128)(2,1)S(1)}, u32[]{:S(2)}, u32[]{:S(2)}) collective-permute-start(bf16[32,56,128]{2,1,0:T(8,128)(2,1)S(1)} %get-tuple-element.28), channel_id=1, source_target_pairs={{0,1},{1,0},{2,3},{3,2},{4,5},{5,4},{6,7},{7,6},{8,9},{9,8},{10,11... | collective-permute-start | bytes 1376264 | tf_op jit(solution)/shard_map/ppermute | solution.py:548

commit v5 on v4

--- a/solution.py
+++ b/solution.py
@@ -77,7 +77,15 @@
     return ones_where(head_of_lane(k) == 2 * pair + (lane >> 6), bf16)
 
 
-def pack_kernel(core_ref, bc_ref, dt_ref, out_ref):
+def pack_kernel(core_ref, bc_hbm, dt_hbm, out_ref, bc_ref, dt_ref, sems):
+    copies = [
+        pltpu.make_async_copy(bc_hbm, bc_ref, sems.at[0]),
+        pltpu.make_async_copy(dt_hbm, dt_ref, sems.at[1]),
+    ]
+    for copy in copies:
+        copy.start()
+    for copy in copies:
+        copy.wait()
     bc = bc_ref[...].astype(f32)
     row, lane = iota((HEADS, LANES), 0), iota((HEADS, LANES), 1)
     dt = [mm(dt_ref[...], ones_where(lane == row + 40 * k), TN) for k in range(3)]
@@ -236,7 +244,10 @@
     return jnp.maximum(pre, 0.0) + jnp.log1p(jnp.exp(-jnp.abs(pre)))
 
 
-def inside_kernel(small_ref, x_ref, g_ref, after_ref, scaled_hbm, sums_ref, scaled_ref, sem):
+def inside_kernel(
+    small_ref, x_ref, g_ref, skip_ref, after_ref,
+    base_hbm, sums_ref, lines_hbm, base_ref, lines_ref, sems,
+):
     proj, cum = small_ref[0], small_ref[2]
     step = softplus(small_ref[1])
     row, lane = iota((LANES, LANES), 0), iota((LANES, LANES), 1)
@@ -250,6 +261,15 @@
     across = jnp.zeros((TOK, TOK), f32)
     own = jnp.zeros((TOK, LANES), f32)
     sums_ref[2] = jnp.zeros((LANES, TOK), f32)
+    stacked = jnp.concatenate(
+        [
+            split(step),
+            split(step * jnp.exp(cum[TOK - 1 : TOK] - cum)),
+            split(jnp.exp(cum)),
+            split(jnp.broadcast_to(triple(skip_ref[...]), (16, LANES))),
+        ],
+        axis=0,
+    )
     first_half = ones_where(lane < 64, bf16)
     second_half = ones_where(lane >= 64, bf16)
     for pair in range(PAIRS):
@@ -270,25 +290,40 @@
             sums_ref[2, head : head + 1, :] = jnp.sum(product * step_col, axis=0, keepdims=True)
             mixed.append((meet * weight).astype(bf16))
             parts.append(g_half)
-        scaled_ref[:, cols] = lax.dot_general(
+        scaled = lax.dot_general(
             jnp.concatenate(mixed, axis=1), jnp.concatenate(parts, axis=0), NN,
             preferred_element_type=f32,
         )
+        wide = lax.dot_general(stacked, spread_matrix(pair), NN, preferred_element_type=f32)
+        x, g = x.astype(f32), g.astype(f32)
+        base_ref[:, cols] = g * wide[3 * TOK : 3 * TOK + 1] + wide[0:TOK] * scaled
+        high, low_part = high_low(
+            jnp.concatenate([g * wide[2 * TOK : 3 * TOK], x * wide[TOK : 2 * TOK]], axis=0)
+        )
+        lines_ref[:, cols] = high
+        lines_ref[:, WIDE + LANES * pair : WIDE + LANES * pair + LANES] = low_part
     sums_ref[0] = across
     sums_ref[1] = own
-    store = pltpu.make_async_copy(scaled_ref, scaled_hbm, sem)
-    store.start()
-    store.wait()
+    copies = [
+        pltpu.make_async_copy(base_ref, base_hbm, sems.at[0]),
+        pltpu.make_async_copy(lines_ref, lines_hbm, sems.at[1]),
+    ]
+    for copy in copies:
+        copy.start()
+    for copy in copies:
+        copy.wait()
 
 
 def last_kernel(
-    core_ref, carried_ref, other_ref, small_ref, scaled_hbm, inner_ref, turned_ref, x_ref, g_ref,
-    rate_ref, skip_ref,
+    core_ref, carried_ref, other_ref, small_ref, base_hbm, inner_ref, lines_hbm, turned_ref,
+    x_ref, g_ref, rate_ref,
     grads_ref, head_grad_ref, keep_ref, send_ref,
-    scaled_ref, state_all, lines_all, terms_all, select_all, sem,
+    base_ref, state_all, lines_all, terms_all, select_all, sems,
 ):
-    fetch = pltpu.make_async_copy(scaled_hbm, scaled_ref, sem)
-    fetch.start()
+    fetch_base = pltpu.make_async_copy(base_hbm, base_ref, sems.at[0])
+    fetch_base.start()
+    fetch_lines = pltpu.make_async_copy(lines_hbm, lines_all, sems.at[1])
+    fetch_lines.start()
     proj, pre, cum = small_ref[0], small_ref[1], small_ref[2]
     step = softplus(pre)
     total = cum[TOK - 1 : TOK]
@@ -302,10 +337,9 @@
     left = jnp.concatenate(high_low(left), axis=0)
     stacked = jnp.concatenate(
         [
-            split(step),
+            split(step * jnp.exp(total - cum)),
             split(jnp.exp(total - cum)),
             split(jnp.exp(cum)),
-            split(jnp.broadcast_to(triple(skip_ref[...]), (16, LANES))),
         ],
         axis=0,
     )
@@ -328,17 +362,13 @@
         wide = lax.dot_general(
             stacked, spread_matrix(2 * two, 2), NN, preferred_element_type=f32
         )
-        step_w, end_w, start_w = wide[0:TOK], wide[TOK : 2 * TOK], wide[2 * TOK : 3 * TOK]
-        skip_w = wide[3 * TOK : 3 * TOK + 1]
+        push_w, end_w, start_w = wide[0:TOK], wide[TOK : 2 * TOK], wide[2 * TOK :]
         x, g = x_ref[:, cols].astype(f32), g_ref[:, cols].astype(f32)
         weighted = g * start_w
         ending = x * end_w
         pushed = lax.dot_general(left, state_b, NN, preferred_element_type=f32)
         pushed = pushed[0 : 2 * TOK] + pushed[2 * TOK :]
         out, reach = pushed[0:TOK], pushed[TOK:]
-        high, low_part = high_low(jnp.concatenate([weighted, ending * step_w], axis=0))
-        lines_all[:, cols] = high
-        lines_all[:, later_cols] = low_part
         pairing = jnp.sum((state_in * state_grad).reshape(CHIPS, 8, 2 * LANES), axis=0)
         pairing = jnp.concatenate([pairing, jnp.zeros((8, 2 * LANES), f32)], axis=0)
         high, low_part = high_low(
@@ -347,15 +377,15 @@
         terms_all[:, cols] = high
         terms_all[:, later_cols] = low_part
         if two == 0:
-            fetch.wait()
-        whole = scaled_ref[:, cols] + end_w * reach
-        head_grad_ref[:, cols] = (g * skip_w + step_w * whole).astype(bf16)
+            fetch_base.wait()
+        head_grad_ref[:, cols] = (base_ref[:, cols] + push_w * reach).astype(bf16)
 
     def both_parts(ref, right, dims):
         return lax.dot_general(
             ref[:, 0:WIDE], right, dims, preferred_element_type=f32
         ) + lax.dot_general(ref[:, WIDE:], right, dims, preferred_element_type=f32)
 
+    fetch_lines.wait()
     crossed = both_parts(lines_all, state_all[...], NT)
     sums = both_parts(terms_all, select_all[...], NN)
     through, reached = sums[0:TOK], sums[TOK : 2 * TOK]
@@ -482,7 +512,11 @@
     three = shape((3, TOK, LANES), f32)
     dma = pltpu.SemaphoreType.DMA
 
-    sent = call(pack_kernel, "pack", chunks, [core], [bc_weight, dt_weight.T])
+    sent = call(
+        pack_kernel, "pack", chunks, [core], [bc_weight, dt_weight.T],
+        in_hbm=(0, 1),
+        scratch=[pltpu.VMEM((ROWS, LANES), bf16), pltpu.VMEM((HEADS, ROWS), bf16), dma((2,))],
+    )
     mine = lax.all_to_all(sent, "dp", 0, 0, tiled=True)
     other = lax.ppermute(mine, "seq", SWAP)
     weight, small, held, leaving = call(
@@ -510,15 +544,19 @@
     states = shape((CHIPS, 160, LANES), bf16)
     entering = call(chain_kernel, "chain", states, [core], [gathered])
     carried = same_core_all_to_all(entering)
-    scaled, inner = call(
+    base, inner, lines = call(
         inside_kernel,
         "inside",
-        (shape((TOK, WIDE), f32), three),
+        (shape((TOK, WIDE), f32), three, shape((2 * TOK, 2 * WIDE), bf16)),
         [],
-        [small, x, g],
-        out_hbm=(0,),
+        [small, x, g, skip],
+        out_hbm=(0, 2),
         after=[entering],
-        scratch=[pltpu.VMEM((TOK, WIDE), f32), dma],
+        scratch=[
+            pltpu.VMEM((TOK, WIDE), f32),
+            pltpu.VMEM((2 * TOK, 2 * WIDE), bf16),
+            dma((2,)),
+        ],
         cost=(400_000_000, 4_000_000),
     )
     passed = call(pass_kernel, "pass", states, [], [carried, held, small], after=[inner])
@@ -534,15 +572,15 @@
             chunks,
         ),
         [core],
-        [carried, other_carried, small, scaled, inner, turned, x, g, rate, skip],
-        in_hbm=(3,),
+        [carried, other_carried, small, base, inner, lines, turned, x, g, rate],
+        in_hbm=(3, 5),
         scratch=[
             pltpu.VMEM((TOK, WIDE), f32),
             pltpu.VMEM((LANES, WIDE), bf16),
             pltpu.VMEM((2 * TOK, 2 * WIDE), bf16),
             pltpu.VMEM((2 * TOK + 16, 2 * WIDE), bf16),
             pltpu.VMEM((WIDE, LANES), bf16),
-            dma,
+            dma((2,)),
         ],
     )
     other = lax.ppermute(send, "seq", SWAP)

time: 135 us -> 134 us (level)
  local copies, waits for them, and re-layouts: 1.55 us -> 0.03 us
  Pallas kernels: 20.6 us -> 22 us
    unnamed x18 -> x14, local copies, waits for them, and re-layouts: 1.55 us -> 0.03 us
    pallas_call x11, Pallas kernels: 20.6 us -> 22 us  [call(): pl.pallas_call(kernel, name=name, out_shape=out_shape, in_specs=[smem] *...]
  transfers between devices with their start and end apart: 5 -> 5, of which waited for: 4 -> 4; matrix products, arithmetic and copies ran while one was open for 0% -> 0% of each run, Pallas kernels for 5% -> 6%
where the time goes in v5:
time: 134 us; the launch traced here: 133 us
  blocking collectives  84.5 us (63%)
  Pallas kernels  22 us (16%)
  starting transfers between devices  17.8 us (13%)
  waiting for transfers between devices  8.32 us (6%)
    all_to_all x1, blocking collectives, body(): mine = lax.all_to_all(sent, 'dp', 0, 0, tiled=True)  24.1 us
    all_to_all x1, blocking collectives, same_core_all_to_all(): lax.all_to_all(value, 'seq', 0, 0, axis_index_groups=CORES, tiled=True)  22.9 us
    pallas_call x11, Pallas kernels, call(): pl.pallas_call(kernel, name=name, out_shape=out_shape, in_specs=[smem] *...  22 us
    all_to_all x1, blocking collectives, body(): owned = lax.all_to_all(paired, 'dp', 0, 0, tiled=True)  19.2 us
    all_gather x1, blocking collectives, body(): parts = lax.all_gather(owned, 'seq')  18.3 us
    ppermute x1, starting transfers between devices, body(): other_carried = lax.ppermute(passed, 'seq', SWAP)  5.19 us
    ppermute x1, starting transfers between devices, body(): other = lax.ppermute(mine, 'seq', SWAP)  4.59 us
    all_to_all x1, waiting for transfers between devices, same_core_all_to_all(): lax.all_to_all(value, 'seq', 0, 0, axis_index_groups=CORES, tiled=True)  4.3 us
  transfers between devices with their start and end apart: 5, of which 4 were waited for; matrix products, arithmetic and copies ran while one was open for 0% of the time, Pallas kernels for 6%

profile of v5, /device:TPU:9, one launch (start us, length us, event | category | flops | bytes accessed | tf_op | source)
XLA Modules:
  0.0 133.5 jit_solution(12965901011128514810)
XLA Ops:
  0.7 1.1 pack.1
  1.8 24.1 %all_to_all.20.mine_ref = bf16[32,56,128]{2,1,0:T(8,128)(2,1)S(1)} all-to-all(bf16[32,56,128]{2,1,0:T(8,128)(2,1)S(1)} %pack.1), channel_id=1, replica_groups=mesh['dp'=32,'seq'=16] {'dp'}, dimensions={0} | all-to-all | bytes 917504 | tf_op jit(solution)/shard_map/all_to_all | solution.py:520
  25.9 4.6 %collective-permute-start = (bf16[32,56,128]{2,1,0:T(8,128)(2,1)S(1)}, bf16[32,56,128]{2,1,0:T(8,128)(2,1)S(1)}, u32[]{:S(2)}, u32[]{:S(2)}) collective-permute-start(bf16[32,56,128]{2,1,0:T(8,128)(2,1)S(1)} %all_to_all.20.mine_ref), channel_id=1, source_target_pairs={{0,1},{1,0},{2,3},{3,2},{4,5},{5,4},{6,7},{7,6},{8,9},{9,8},{10,11... | collective-permute-start | bytes 1376264 | tf_op jit(solution)/shard_map/ppermute | solution.py:521
  30.5 1.4 %collective-permute-done.other_ref = bf16[32,56,128]{2,1,0:T(8,128)(2,1)S(1)} collective-permute-done((bf16[32,56,128]{2,1,0:T(8,128)(2,1)S(1)}, bf16[32,56,128]{2,1,0:T(8,128)(2,1)S(1)}, u32[]{:S(2)}, u32[]{:S(2)}) %collective-permute-start) | collective-permute-done | bytes 458784 | tf_op jit(solution)/shard_map/ppermute | solution.py:521
  31.9 4.2 %first.1 = (bf16[2560,256]{1,0:T(8,128)(2,1)}, f32[3,128,128]{2,1,0:T(8,128)S(1)}, f32[8,160,128]{2,1,0:T(8,128)S(1)}, f32[8,168,128]{2,1,0:T(8,128)S(1)}) custom-call(s32[1]{0:T(128)} %bitcast.core_ref, bf16[32,56,128]{2,1,0:T(8,128)(2,1)S(1)} %all_to_all.20.mine_ref, bf16[32,56,128]{2,1,0:T(8,128)(2,1)S(1)} %collective-permute-done.other_ref, ...), custom_call_target="tpu_custom_call" | custom-call | tf_op jit(solution)/shard_map/first/pallas_call | solution.py:481
  36.2 2.3 %collective-permute-start.1 = (f32[8,168,128]{2,1,0:T(8,128)S(1)}, f32[8,168,128]{2,1,0:T(8,128)S(1)}, u32[]{:S(2)}, u32[]{:S(2)}) collective-permute-start(f32[8,168,128]{2,1,0:T(8,128)S(1)} %get-tuple-element.20), channel_id=1, source_target_pairs={{0,1},{1,0},{2,3},{3,2},{4,5},{5,4},{6,7},{7,6},{8,9},{9,8},{10,11... | collective-permute-start | bytes 2064392 | tf_op jit(solution)/shard_map/ppermute | solution.py:541
  38.5 1.7 %collective-permute-done.1.other_ref = f32[8,168,128]{2,1,0:T(8,128)S(1)} collective-permute-done((f32[8,168,128]{2,1,0:T(8,128)S(1)}, f32[8,168,128]{2,1,0:T(8,128)S(1)}, u32[]{:S(2)}, u32[]{:S(2)}) %collective-permute-start.1) | collective-permute-done | bytes 688160 | tf_op jit(solution)/shard_map/ppermute | solution.py:541
  40.2 0.2 chip.1
  40.5 22.9 %all_to_all.21.state_ref = bf16[8,168,128]{2,1,0:T(8,128)(2,1)S(1)} all-to-all(bf16[8,168,128]{2,1,0:T(8,128)(2,1)S(1)} %chip.1), channel_id=1, replica_groups={{0,2,4,6,8,10,12,14},{1,3,5,7,9,11,13,15},{16,18,20,22,24,26,28,30},{17..., dimensions={0} | all-to-all | bytes 688128 | tf_op jit(solution)/shard_map/all_to_all | solution.py:504
  63.3 1.1 chain.1.after_ref
  64.4 3.4 %all-to-all-start.2 = ((bf16[8,160,128]{2,1,0:T(8,128)(2,1)}), bf16[8,160,128]{2,1,0:T(8,128)(2,1)S(1)}, u32[]{:S(2)}, u32[]{:S(2)}) async-start(bf16[8,160,128]{2,1,0:T(8,128)(2,1)} %chain.1.after_ref), calls=%async_computation.2 | async-start | bytes 655360 | tf_op jit(solution)/shard_map/all_to_all | solution.py:504
  67.8 6.7 %inside.1 = (f32[128,2560]{1,0:T(8,128)}, f32[3,128,128]{2,1,0:T(8,128)S(1)}, bf16[256,5120]{1,0:T(8,128)(2,1)}) custom-call(f32[3,128,128]{2,1,0:T(8,128)S(1)} %get-tuple-element.21.small_ref, bf16[128,2560]{1,0:T(8,128)(2,1)S(1)} %bitcast.13, bf16[128,2560]{1,0:T(8,128)(2,1)S(1)} %bitcast.16, f32[1,40]{1,0:T(1,128)S(1)} %bitcast.24, ...), custom_call_target="tpu_custom_call" | custom-call | flops 400000000 | bytes 4000000 | tf_op jit(solution)/shard_map/inside/pallas_call | solution.py:481
  74.6 4.3 %all-to-all-done.2.carried_ref = bf16[8,160,128]{2,1,0:T(8,128)(2,1)S(1)} async-done(((bf16[8,160,128]{2,1,0:T(8,128)(2,1)}), bf16[8,160,128]{2,1,0:T(8,128)(2,1)S(1)}, u32[]{:S(2)}, u32[]{:S(2)}) %all-to-all-start.2) | async-done | bytes 327712 | tf_op jit(solution)/shard_map/all_to_all | solution.py:504
  78.9 0.2 pass.1
  79.1 5.2 %collective-permute-start.2 = (bf16[8,160,128]{2,1,0:T(8,128)(2,1)S(1)}, bf16[8,160,128]{2,1,0:T(8,128)(2,1)S(1)}, u32[]{:S(2)}, u32[]{:S(2)}) collective-permute-start(bf16[8,160,128]{2,1,0:T(8,128)(2,1)S(1)} %pass.1), channel_id=1, source_target_pairs={{0,1},{1,0},{2,3},{3,2},{4,5},{5,4},{6,7},{7,6},{8,9},{9,8},{10,11... | collective-permute-start | bytes 983048 | tf_op jit(solution)/shard_map/ppermute | solution.py:563
  84.3 0.2 turn.1.turned_ref
  84.5 0.8 collective-permute-done.2.other_ref
  85.4 5.9 %last.1 = (bf16[256,256]{1,0:T(8,128)(2,1)S(1)}, bf16[128,2560]{1,0:T(8,128)(2,1)}, f32[32,56,128]{2,1,0:T(8,128)S(1)}, bf16[32,56,128]{2,1,0:T(8,128)(2,1)S(1)}) custom-call(s32[1]{0:T(128)} %bitcast.core_ref, bf16[8,160,128]{2,1,0:T(8,128)(2,1)S(1)} %all-to-all-done.2.carried_ref, bf16[8,160,128]{2,1,0:T(8,128)(2,1)S(1)} %collective-permute-done.2.other_ref, ...), custom_call_target="tpu_custom_call" | custom-call | tf_op jit(solution)/shard_map/last/pallas_call | solution.py:481
  91.2 2.3 %collective-permute-start.3 = (bf16[32,56,128]{2,1,0:T(8,128)(2,1)S(1)}, bf16[32,56,128]{2,1,0:T(8,128)(2,1)S(1)}, u32[]{:S(2)}, u32[]{:S(2)}) collective-permute-start(bf16[32,56,128]{2,1,0:T(8,128)(2,1)S(1)} %get-tuple-element.30), channel_id=1, source_target_pairs={{0,1},{1,0},{2,3},{3,2},{4,5},{5,4},{6,7},{7,6},{8,9},{9,8},{10,11... | collective-permute-start | bytes 1376264 | tf_op jit(solution)/shard_map/ppermute | solution.py:586
  93.5 1.4 %back.1 = (bf16[128,2560]{1,0:T(8,128)(2,1)}, f32[8,128]{1,0:T(8,128)S(1)}) custom-call(bf16[256,256]{1,0:T(8,128)(2,1)S(1)} %get-tuple-element.25.grads_ref, bf16[2560,256]{1,0:T(8,128)(2,1)S(1)} %copy-done.3), custom_call_target="tpu_custom_call" | custom-call | flops 340000000 | bytes 3000000 | tf_op jit(solution)/shard_map/back/pallas_call | solution.py:481
  94.9 0.1 join.1
  95.0 19.2 %all_to_all.22 = bf16[32,56,128]{2,1,0:T(8,128)(2,1)S(1)} all-to-all(bf16[32,56,128]{2,1,0:T(8,128)(2,1)S(1)} %join.1), channel_id=1, replica_groups=mesh['dp'=32,'seq'=16] {'dp'}, dimensions={0} | all-to-all | bytes 917504 | tf_op jit(solution)/shard_map/all_to_all | solution.py:596
  114.3 18.3 %all-gather = f32[896,128]{1,0:T(8,128)S(1)} all-gather(f32[56,128]{1,0:T(8,128)S(1)} %convert_reduce_fusion), channel_id=2, replica_groups=mesh['dp'=32,'seq'=16] {'seq'}, dimensions={0}, use_global_device_ids=true | all-gather | bytes 487424 | tf_op jit(solution)/shard_map/all_gather | solution.py:598
  132.6 0.9 finish.1
  (16 shorter events, 0.1 us)
Async XLA Ops:
  0.6 31.3 %copy-start.4 = (f32[40]{0:T(128)S(1)}, f32[40]{0:T(128)}, u32[]{:S(2)}) copy-start(f32[40]{0:T(128)} %param.14) | copy-start | bytes 484
  0.6 31.3 %copy-start.5 = (f32[40]{0:T(128)S(1)}, f32[40]{0:T(128)}, u32[]{:S(2)}) copy-start(f32[40]{0:T(128)} %param.13) | copy-start | bytes 484
  0.7 31.3 %copy-start.1 = (bf16[1,128,2560]{2,1,0:T(8,128)(2,1)S(1)}, bf16[1,128,2560]{2,1,0:T(8,128)(2,1)}, u32[]{:S(2)}) copy-start(bf16[1,128,2560]{2,1,0:T(8,128)(2,1)} %param.10) | copy-start | bytes 1966084
  0.7 31.3 %copy-start = (bf16[1,128,2560]{2,1,0:T(8,128)(2,1)S(1)}, bf16[1,128,2560]{2,1,0:T(8,128)(2,1)}, u32[]{:S(2)}) copy-start(bf16[1,128,2560]{2,1,0:T(8,128)(2,1)} %param.9) | copy-start | bytes 1966084
  25.9 6.0 %collective-permute-start = (bf16[32,56,128]{2,1,0:T(8,128)(2,1)S(1)}, bf16[32,56,128]{2,1,0:T(8,128)(2,1)S(1)}, u32[]{:S(2)}, u32[]{:S(2)}) collective-permute-start(bf16[32,56,128]{2,1,0:T(8,128)(2,1)S(1)} %all_to_all.20.mine_ref), channel_id=1, source_target_pairs={{0,1},{1,0},{2,3},{3,2},{4,5},{5,4},{6,7},{7,6},{8,9},{9,8},{10,11... | collective-permute-start | bytes 1376264 | tf_op jit(solution)/shard_map/ppermute | solution.py:521
  36.2 4.0 %collective-permute-start.1 = (f32[8,168,128]{2,1,0:T(8,128)S(1)}, f32[8,168,128]{2,1,0:T(8,128)S(1)}, u32[]{:S(2)}, u32[]{:S(2)}) collective-permute-start(f32[8,168,128]{2,1,0:T(8,128)S(1)} %get-tuple-element.20), channel_id=1, source_target_pairs={{0,1},{1,0},{2,3},{3,2},{4,5},{5,4},{6,7},{7,6},{8,9},{9,8},{10,11... | collective-permute-start | bytes 2064392 | tf_op jit(solution)/shard_map/ppermute | solution.py:541
  40.5 27.4 %copy-start.6 = (f32[40]{0:T(128)S(1)}, f32[40]{0:T(128)}, u32[]{:S(2)}) copy-start(f32[40]{0:T(128)} %param.15) | copy-start | bytes 484
  64.4 14.5 %all-to-all-start.2 = ((bf16[8,160,128]{2,1,0:T(8,128)(2,1)}), bf16[8,160,128]{2,1,0:T(8,128)(2,1)S(1)}, u32[]{:S(2)}, u32[]{:S(2)}) async-start(bf16[8,160,128]{2,1,0:T(8,128)(2,1)} %chain.1.after_ref), calls=%async_computation.2 | async-start | bytes 655360 | tf_op jit(solution)/shard_map/all_to_all | solution.py:504
  74.6 9.8 %copy-start.2 = (bf16[1,128,2560]{2,1,0:T(8,128)(2,1)S(1)}, bf16[1,128,2560]{2,1,0:T(8,128)(2,1)}, u32[]{:S(2)}) copy-start(bf16[1,128,2560]{2,1,0:T(8,128)(2,1)} %param.8) | copy-start | bytes 1966084
  79.1 6.3 %collective-permute-start.2 = (bf16[8,160,128]{2,1,0:T(8,128)(2,1)S(1)}, bf16[8,160,128]{2,1,0:T(8,128)(2,1)S(1)}, u32[]{:S(2)}, u32[]{:S(2)}) collective-permute-start(bf16[8,160,128]{2,1,0:T(8,128)(2,1)S(1)} %pass.1), channel_id=1, source_target_pairs={{0,1},{1,0},{2,3},{3,2},{4,5},{5,4},{6,7},{7,6},{8,9},{9,8},{10,11... | collective-permute-start | bytes 983048 | tf_op jit(solution)/shard_map/ppermute | solution.py:563
  85.4 8.2 %copy-start.3 = (bf16[2560,256]{1,0:T(8,128)(2,1)S(1)}, bf16[2560,256]{1,0:T(8,128)(2,1)}, u32[]{:S(2)}) copy-start(bf16[2560,256]{1,0:T(8,128)(2,1)} %get-tuple-element.26.weight_ref) | copy-start | bytes 3932164
  91.2 3.7 %collective-permute-start.3 = (bf16[32,56,128]{2,1,0:T(8,128)(2,1)S(1)}, bf16[32,56,128]{2,1,0:T(8,128)(2,1)S(1)}, u32[]{:S(2)}, u32[]{:S(2)}) collective-permute-start(bf16[32,56,128]{2,1,0:T(8,128)(2,1)S(1)} %get-tuple-element.30), channel_id=1, source_target_pairs={{0,1},{1,0},{2,3},{3,2},{4,5},{5,4},{6,7},{7,6},{8,9},{9,8},{10,11... | collective-permute-start | bytes 1376264 | tf_op jit(solution)/shard_map/ppermute | solution.py:586
